TPU v7x, 512 devices: a whole 4x4x16 slice. The times are simulated.
512 devices in a mesh: space: 16 (over y, x_hi, core), date: 32 (over x_lo, z).
Axes of the slice: x: 4 (x_hi: 2, x_lo: 2; x = x_hi * 2 + x_lo), y: 4, z: 16, core: 2. Of those that a mesh axis runs over, the one named last changes fastest.
Arguments:
- obs: bfloat16 [7, 768, 128, 512], P(None, 'date', 'space'), may hold values from -30 to 30
- valid: int32 [768, 128, 512], P('date', 'space'), may hold values from 0 to 1
- days: int32 [768], P('date'), may hold values from 0 to 3649, as said below
Outputs:
- coefficients: float32 [7, 8, 128, 512], P(None, None, 'space', 'date')
- noise_scale: float32 [128, 512], P('space', 'date')
Inputs may be any that keep to these rules, and one draw needn't show every extreme that they name: `days`: day numbers of the acquisitions, in no particular order.
All inputs are finite; a program needn't handle non-finite values.
Results may differ from a plain program's by a relative error of at most 0.0003.
Values may be sent and summed in bfloat16 or wider, within the bound.
A program may use at most 128 MiB of HBM per device.

v0:
```python
import math

import jax
import jax.numpy as jnp
import numpy as np
from jax import lax
from jax.sharding import PartitionSpec as P

ITERS = 2


tukey_const = 4.685
ridge_value = 1.0
scale_eps = 1e-06
highest = lax.Precision.HIGHEST
pair_first = np.array(
    [row_index for row_index in range(8) for col_index in range(row_index, 8)], dtype=np.int32
)
pair_second = np.array(
    [col_index for row_index in range(8) for col_index in range(row_index, 8)], dtype=np.int32
)


def padded_2(block, sides, width):
    for axis, dim in sides:
        count = lax.axis_size(axis)
        forward = [(i, i + 1) for i in range(count - 1)]
        backward = [(target, source) for source, target in forward]
        low = lax.ppermute(
            lax.slice_in_dim(block, block.shape[dim] - width, None, axis=dim), axis, forward
        )
        high = lax.ppermute(lax.slice_in_dim(block, 0, width, axis=dim), axis, backward)
        block = jnp.concatenate([low, block, high], axis=dim)
    return block


def design(day_numbers):
    day_float = day_numbers.astype(jnp.float32)
    columns = [jnp.ones_like(day_float), (day_float - 1825.0) / 1825.0]
    angle = day_float * (2.0 * math.pi / 365.25)
    for harmonic in range(1, 4):
        columns.append(jnp.cos(harmonic * angle))
        columns.append(jnp.sin(harmonic * angle))
    return jnp.stack(columns, axis=1)


def form_moments(design_rows, weighted, observed):
    products = design_rows[:, pair_first] * design_rows[:, pair_second]
    gram_terms = jnp.dot(
        products.T, weighted, precision=highest, preferred_element_type=jnp.float32
    )
    cross_terms = jnp.einsum(
        "dk,bdp->bkp",
        design_rows,
        weighted[None] * observed,
        precision=highest,
        preferred_element_type=jnp.float32,
    )
    return jnp.concatenate([gram_terms, cross_terms.reshape(-1, weighted.shape[1])], axis=0)


def solve_terms(summed, band_count):
    term_count = 8
    entries = {}
    position = 0
    for row_index in range(term_count):
        for col_index in range(row_index, term_count):
            entries[row_index, col_index] = summed[position]
            position += 1
    right_sides = summed[position:].reshape((band_count, term_count) + summed.shape[1:])
    lower_factor = {}
    for col_index in range(term_count):
        pivot_value = entries[col_index, col_index] + ridge_value
        for inner_index in range(col_index):
            pivot_value = (
                pivot_value
                - lower_factor[col_index, inner_index] * lower_factor[col_index, inner_index]
            )
        pivot_root = jnp.sqrt(pivot_value)
        lower_factor[col_index, col_index] = pivot_root
        for row_index in range(col_index + 1, term_count):
            entry_value = entries[col_index, row_index]
            for inner_index in range(col_index):
                entry_value = (
                    entry_value
                    - lower_factor[row_index, inner_index] * lower_factor[col_index, inner_index]
                )
            lower_factor[row_index, col_index] = entry_value / pivot_root
    forward = []
    for row_index in range(term_count):
        running = right_sides[:, row_index]
        for inner_index in range(row_index):
            running = running - lower_factor[row_index, inner_index][None] * forward[inner_index]
        forward.append(running / lower_factor[row_index, row_index][None])
    solved = [None] * term_count
    for row_index in reversed(range(term_count)):
        running = forward[row_index]
        for inner_index in range(row_index + 1, term_count):
            running = running - lower_factor[inner_index, row_index][None] * solved[inner_index]
        solved[row_index] = running / lower_factor[row_index, row_index][None]
    return (jnp.stack(solved, axis=1), entries[0, 0])


def residual_power(design_rows, observed, coefficient):
    fitted = jnp.einsum(
        "dk,bkp->bdp",
        design_rows,
        coefficient,
        precision=highest,
        preferred_element_type=jnp.float32,
    )
    misfit = observed - fitted
    return jnp.mean(misfit * misfit, axis=0)


def box_sum(padded, row_count, col_count):
    across = padded[0:row_count]
    for offset in range(1, 5):
        across = across + padded[offset : offset + row_count]
    window_sum = across[:, 0:col_count]
    for offset in range(1, 5):
        window_sum = window_sum + across[:, offset : offset + col_count]
    return window_sum


def window_counts(first_index, length, whole):
    global_index = first_index + jnp.arange(length, dtype=jnp.int32)
    return (jnp.minimum(global_index + 2, whole - 1) - jnp.maximum(global_index - 2, 0) + 1).astype(
        jnp.float32
    )


def spread_rows(spread, weight_total, row_count, col_count):
    full_spread = lax.psum(spread, "date")
    variance = full_spread / (1.0 + weight_total)
    padded = padded_2(variance.reshape(row_count, col_count), (("space", 0),), 2)
    return jnp.pad(padded, ((0, 0), (2, 2)))


def next_weight(resid_power, smooth, mask_float):
    scaled = jnp.minimum(
        resid_power / (tukey_const * tukey_const * (smooth[None] + scale_eps)), 1.0
    )
    return mask_float * (1.0 - scaled) * (1.0 - scaled)


def on_device(obs, valid, days):
    band_count, date_count, row_count, col_count = obs.shape
    date_devices = lax.axis_size("date")
    date_index = lax.axis_index("date")
    cols_local = col_count // date_devices
    row_first = lax.axis_index("space") * row_count
    grid_rows = row_count * lax.axis_size("space")
    pixels = row_count * col_count
    mask_float = valid.astype(jnp.float32).reshape(date_count, pixels)
    observed = obs.astype(jnp.float32).reshape(band_count, date_count, pixels)
    design_rows = design(days)
    col_first = 0
    slice_start = date_index * cols_local
    counts = (
        window_counts(row_first, row_count, grid_rows)[:, None]
        * window_counts(col_first, col_count, col_count)[None, :]
    )
    weighted = mask_float
    for step in range(ITERS):
        local_terms = form_moments(design_rows, weighted, observed)
        summed = lax.psum(local_terms, "date")
        coefficient, weight_total = solve_terms(summed, band_count)
        resid_power = residual_power(design_rows, observed, coefficient)
        spread = jnp.sum(weighted * resid_power, axis=0)
        padded = spread_rows(spread, weight_total, row_count, col_count)
        smooth = (box_sum(padded, row_count, col_count) / counts).reshape(pixels)
        if step + 1 < ITERS:
            weighted = next_weight(resid_power, smooth, mask_float)
    coefficient = coefficient.reshape(band_count, 8, row_count, col_count)
    noise_scale = jnp.sqrt(smooth + scale_eps).reshape(row_count, col_count)
    coefficients = lax.dynamic_slice_in_dim(coefficient, slice_start, cols_local, 3)
    noise_block = lax.dynamic_slice_in_dim(noise_scale, slice_start, cols_local, 1)
    return (coefficients, noise_block)


def solution(mesh):
    in_specs = (P(None, "date", "space", None), P("date", "space", None), P("date"))
    out_specs = (P(None, None, "space", "date"), P("space", "date"))
    return jax.shard_map(
        on_device, mesh=mesh, in_specs=in_specs, out_specs=out_specs, check_vma=False
    )
```

profile of v0, /device:TPU:1, one launch (start us, length us, event | category | flops | bytes accessed | tf_op | source)
XLA Modules:
  0.0 877.3 jit_solution(6437620720839090686)
XLA Ops:
  7.2 0.7 sine_bitcast_fusion
  7.9 0.7 pad_clamp_fusion
  8.6 0.6 gather_fusion
  9.2 0.6 gather_fusion.1
  9.8 1.0 convert_element_type.25
  11.1 2.4 reshape.5086
  13.5 0.6 copy-done.15
  14.1 0.6 fusion.190
  14.7 1.6 convolution_bitcast_fusion.3
  16.3 1.3 pad_maximum_fusion
  17.9 245.5 %all-reduce.5.cloned.1.call-done = f32[92,4096]{1,0:T(8,128)} async-done(((f32[92,4096]{1,0:T(8,128)}), f32[92,4096]{1,0:T(8,128)}) %all-reduce.5.cloned.1.call-update) | async-done | bytes 1507344 | tf_op jit(solution)/shard_map/psum | solution.py:167
  263.4 2.4 slice_add_fusion.28
  265.7 1.8 subtract_sqrt_fusion.11
  267.6 1.7 subtract_sqrt_fusion.10
  269.3 1.6 rsqrt_multiply_fusion.9
  270.9 0.4 rsqrt_multiply_fusion.4
  271.4 0.5 sqrt_multiply_fusion.1
  272.4 2.0 subtract_divide_fusion.19
  274.4 3.7 subtract_divide_fusion.11
  278.1 3.7 stack.72
  281.8 3.8 fusion.6
  285.8 0.7 copy-done
  286.6 0.7 copy-done.2
  287.3 0.6 copy.21
  287.9 93.7 %psum.29 = f32[4096]{0:T(1024)} all-reduce(f32[4096]{0:T(1024)} %bitcast.399), channel_id=1, replica_groups=mesh['space'=16,'date'=32] {'date'}, use_global_device_ids=true, to_apply=%region_3.0 | all-reduce | flops 4096 | bytes 32768 | tf_op jit(solution)/shard_map/psum | solution.py:134
  381.6 0.7 div.1531
  382.4 0.6 copy-done.19
  383.0 0.6 slice.432
  383.6 54.4 %collective-permute-start = (f32[2,512]{1,0:T(2,128)}, f32[2,512]{1,0:T(2,128)S(1)}, u32[]{:S(2)}, u32[]{:S(2)}) collective-permute-start(f32[2,512]{1,0:T(2,128)} %slice.432), channel_id=1, source_target_pairs={{0,32},{32,64},{64,96},{96,128},{128,160},{160,192},{192,224},{224... | collective-permute-start | bytes 12296 | tf_op jit(solution)/shard_map/ppermute | solution.py:29
  437.9 0.6 slice.434
  438.5 2.1 collective-permute-start.1
  440.7 0.6 add_convert_fusion
  441.2 1.3 reshape.5080
  442.5 2.6 collective-permute-done.1
  445.2 0.8 select_maximum_fusion.2
  446.0 1.3 broadcast_multiply_fusion.2
  447.3 0.6 copy-done.17
  448.0 1.6 convolution_bitcast_fusion.2
  449.6 0.6 fusion.191
  450.3 1.3 pad_maximum_fusion.1
  451.6 231.3 %all-reduce.7.cloned.1.call-done = f32[92,4096]{1,0:T(8,128)} async-done(((f32[92,4096]{1,0:T(8,128)}), f32[92,4096]{1,0:T(8,128)}) %all-reduce.7.cloned.1.call-update) | async-done | bytes 1507344 | tf_op jit(solution)/shard_map/psum | solution.py:167
  682.9 1.8 slice_add_fusion.16
  684.7 1.9 subtract_sqrt_fusion.5
  686.5 1.7 subtract_sqrt_fusion.4
  688.3 1.6 rsqrt_multiply_fusion.6
  690.3 0.5 sqrt_multiply_fusion
  691.3 3.8 fusion.144
  695.1 1.0 fusion.148
  696.1 1.1 fusion.149
  697.3 1.2 fusion.150
  698.5 1.4 fusion.151
  699.9 1.5 fusion.152
  701.3 1.6 fusion.153
  702.9 0.6 copy-done.6
  703.6 2.1 fusion.154
  705.7 3.6 stack.82
  709.3 3.8 fusion.7
  713.5 0.6 copy-done.1
  714.4 93.7 %psum.31 = f32[4096]{0:T(1024)S(1)} all-reduce(f32[4096]{0:T(1024)S(1)} %bitcast.400), channel_id=1, replica_groups=mesh['space'=16,'date'=32] {'date'}, use_global_device_ids=true, to_apply=%region_7.8 | all-reduce | flops 4096 | bytes 32768 | tf_op jit(solution)/shard_map/psum | solution.py:134
  808.1 54.4 %collective-permute-start.2 = (f32[2,512]{1,0:T(2,128)S(1)}, f32[2,512]{1,0:T(2,128)S(1)}, u32[]{:S(2)}, u32[]{:S(2)}) collective-permute-start(f32[2,512]{1,0:T(2,128)S(1)} %slice.491), channel_id=1, source_target_pairs={{0,32},{32,64},{64,96},{96,128},{128,160},{160,192},{192,224},{224... | collective-permute-start | bytes 12296 | tf_op jit(solution)/shard_map/ppermute | solution.py:29
  862.5 1.9 collective-permute-start.3
  865.1 0.8 constant_dynamic-slice_fusion
  865.9 3.0 collective-permute-done.3
  869.1 1.4 fusion.128
  (84 shorter events, 3.7 us)
Async XLA Ops:
  7.2 256.2 %all-reduce.5.cloned.1.call-start = ((), (), s32[]{:S(2)}) async-start(), calls=%async_computation | async-start | bytes 3145728 | tf_op jit(solution)/shard_map/psum | solution.py:167
  13.5 0.6 copy-start.15
  17.6 665.3 %all-reduce.7.cloned.1.call-start = ((), (), s32[]{:S(2)}) async-start(), calls=%async_computation.1 | async-start | bytes 3145728 | tf_op jit(solution)/shard_map/psum | solution.py:167
  263.4 7.5 copy-start.5
  285.6 1.0 copy-start
  286.6 0.8 copy-start.2
  382.4 0.6 copy-start.19
  383.6 59.0 %collective-permute-start = (f32[2,512]{1,0:T(2,128)}, f32[2,512]{1,0:T(2,128)S(1)}, u32[]{:S(2)}, u32[]{:S(2)}) collective-permute-start(f32[2,512]{1,0:T(2,128)} %slice.432), channel_id=1, source_target_pairs={{0,32},{32,64},{64,96},{96,128},{128,160},{160,192},{192,224},{224... | collective-permute-start | bytes 12296 | tf_op jit(solution)/shard_map/ppermute | solution.py:29
  438.5 6.6 collective-permute-start.1
  447.3 0.6 copy-start.17
  448.0 1.6 copy-start.16
  682.9 7.0 copy-start.4
  702.9 0.6 copy-start.6
  713.1 1.0 copy-start.1
  713.1 1.1 copy-start.3
  713.1 1.1 copy-start.18
  713.1 151.3 %copy-start.11 = (f32[7,4096]{1,0:T(8,128)S(1)}, f32[7,4096]{1,0:T(8,128)}, u32[]{:S(2)}) copy-start(f32[7,4096]{1,0:T(8,128)} %get-tuple-element.23) | copy-start | bytes 344068
  713.1 151.4 %copy-start.10 = (f32[7,4096]{1,0:T(8,128)S(1)}, f32[7,4096]{1,0:T(8,128)}, u32[]{:S(2)}) copy-start(f32[7,4096]{1,0:T(8,128)} %get-tuple-element.21) | copy-start | bytes 344068
  713.1 151.4 %copy-start.14 = (f32[7,4096]{1,0:T(8,128)S(1)}, f32[7,4096]{1,0:T(8,128)}, u32[]{:S(2)}) copy-start(f32[7,4096]{1,0:T(8,128)} %get-tuple-element.19) | copy-start | bytes 344068
  713.2 151.5 %copy-start.9 = (f32[7,4096]{1,0:T(8,128)S(1)}, f32[7,4096]{1,0:T(8,128)}, u32[]{:S(2)}) copy-start(f32[7,4096]{1,0:T(8,128)} %get-tuple-element.17) | copy-start | bytes 344068
  713.2 151.5 %copy-start.13 = (f32[7,4096]{1,0:T(8,128)S(1)}, f32[7,4096]{1,0:T(8,128)}, u32[]{:S(2)}) copy-start(f32[7,4096]{1,0:T(8,128)} %get-tuple-element.15) | copy-start | bytes 344068
  713.2 151.6 %copy-start.8 = (f32[7,4096]{1,0:T(8,128)S(1)}, f32[7,4096]{1,0:T(8,128)}, u32[]{:S(2)}) copy-start(f32[7,4096]{1,0:T(8,128)} %get-tuple-element.13) | copy-start | bytes 344068
  714.2 150.7 %copy-start.12 = (f32[7,4096]{1,0:T(8,128)S(1)}, f32[7,4096]{1,0:T(8,128)}, u32[]{:S(2)}) copy-start(f32[7,4096]{1,0:T(8,128)} %get-tuple-element.11) | copy-start | bytes 344068
  714.2 150.8 %copy-start.7 = (f32[7,4096]{1,0:T(8,128)S(1)}, f32[7,4096]{1,0:T(8,128)}, u32[]{:S(2)}) copy-start(f32[7,4096]{1,0:T(8,128)} %get-tuple-element.2) | copy-start | bytes 344068
  808.1 57.9 %collective-permute-start.2 = (f32[2,512]{1,0:T(2,128)S(1)}, f32[2,512]{1,0:T(2,128)S(1)}, u32[]{:S(2)}, u32[]{:S(2)}) collective-permute-start(f32[2,512]{1,0:T(2,128)S(1)} %slice.491), channel_id=1, source_target_pairs={{0,32},{32,64},{64,96},{96,128},{128,160},{160,192},{192,224},{224... | collective-permute-start | bytes 12296 | tf_op jit(solution)/shard_map/ppermute | solution.py:29
  862.5 6.4 collective-permute-start.3
Sparse Core Ops, SparseCore 0:
  17.7 245.5 all-reduce.4
  451.7 231.1 all-reduce.6
where the time goes:
time: 879 us; the launch traced here: 877 us
  waiting for transfers between devices  482 us (55%)
  blocking collectives  187 us (21%)
  starting transfers between devices  113 us (13%)
  other arithmetic  46.9 us (5%)
  local copies, waits for them, and re-layouts  20.9 us (2%)
  between operations  14.6 us (2%)
  matrix products  12 us (1%)
    psum x2, waiting for transfers between devices, on_device(): summed = lax.psum(local_terms, 'date')  477 us
    psum x2, blocking collectives, spread_rows(): full_spread = lax.psum(spread, 'date')  187 us
    ppermute x2, starting transfers between devices, padded_2(): lax.ppermute(lax.slice_in_dim(block, block.shape[dim] - width, None, axis...  109 us
  transfers between devices with their start and end apart: 6, of which 4 were waited for; matrix products, arithmetic and copies ran while one was open for 0% of the time, Pallas kernels for 0%

commit v1 on v0

v1 whole, which is shorter than its diff:
```python
import functools
import math

import jax
import jax.numpy as jnp
from jax import lax
from jax.experimental import pallas as pl
from jax.experimental.pallas import tpu as pltpu
from jax.sharding import PartitionSpec as P

F32 = jnp.float32
MESH = pl.DeviceIdType.MESH
TUKEY = 4.685
EPS = 1e-06
BANDS = 7
TERMS = 8
ROWS = 8
COLS = 512
TILES = 4
SHARDS = 32
DEEP = 80
HALF = 40
BLOCK = 64
FIELDS = 24
ZS = 16

C0, S0, TC0, TS0, EXTRA_S = 2, 8, 14, 17, 21
NEIGHBOURS = [(a, b) for a in (-1, 0, 1) for b in (-1, 0, 1) if (a, b) != (0, 0)]


def extra_row(e):
    return 8 * e + 7 if e < 8 else 64 + e - 8


def gram_terms(i, j):
    if i > j:
        i, j = j, i
    if i == 0:
        if j < 2:
            return [(1.0, j)]
        n = j // 2
        return [(1.0, (C0 if j % 2 == 0 else S0) + n)]
    if i == 1:
        if j == 1:
            return [(1.0, 2)]
        n = j // 2
        return [(1.0, (TC0 if j % 2 == 0 else TS0) + n)]
    a, b = i // 2, j // 2

    def cosine(n):
        return 0 if n == 0 else C0 + n

    if i % 2 == 0 and j % 2 == 0:
        return [(0.5, cosine(abs(a - b))), (0.5, cosine(a + b))]
    if i % 2 == 1 and j % 2 == 1:
        return [(0.5, cosine(abs(a - b))), (-0.5, cosine(a + b))]
    s, c = (a, b) if i % 2 == 1 else (b, a)
    terms = [(0.5, S0 + s + c)]
    if s != c:
        terms.append((0.5 if s > c else -0.5, S0 + abs(s - c)))
    return terms


def design_table(days):
    day = days.astype(F32)
    angle = day * (2.0 * math.pi / 365.25)
    t = (day - 1825.0) / 1825.0
    c = [None] + [jnp.cos(h * angle) for h in range(1, 4)]
    s = [None] + [jnp.sin(h * angle) for h in range(1, 4)]
    c += [2 * c[2] * c[2] - 1, c[2] * c[3] - s[2] * s[3], 2 * c[3] * c[3] - 1]
    s += [2 * s[2] * c[2], s[2] * c[3] + c[2] * s[3], 2 * s[3] * c[3]]
    fields = [jnp.ones_like(t), t, t * t] + c[1:] + s[1:]
    fields += [t * c[h] for h in range(1, 4)] + [t * s[h] for h in range(1, 4)]
    fields += [jnp.zeros_like(t)] * (FIELDS - len(fields))
    table = jnp.stack(fields, axis=1)
    return jnp.broadcast_to(table.reshape(-1, 1), (table.size, 128))


COLUMN = [0, 1, C0 + 1, S0 + 1, C0 + 2, S0 + 2, C0 + 3, S0 + 3]


def flip_masks():
    sub = lax.broadcasted_iota(jnp.int32, (8, 128), 0)
    group = lax.broadcasted_iota(jnp.int32, (8, 128), 1) // 16
    masks = []
    for bit in (4, 2, 1):
        s, g = (sub & bit) != 0, (group & bit) != 0
        masks.append((jnp.logical_and(s, jnp.logical_not(g)), jnp.logical_and(jnp.logical_not(s), g)))
    return masks


def flip(v, masks):
    for bit, (low, high) in zip((4, 2, 1), masks):
        up = pltpu.roll(pltpu.roll(v, bit, 0), 128 - 16 * bit, 1)
        if bit == 4:
            v = jnp.where(jnp.logical_or(low, high), up, v)
        else:
            down = pltpu.roll(pltpu.roll(v, 8 - bit, 0), 16 * bit, 1)
            v = jnp.where(low, up, jnp.where(high, down, v))
    return v


def tile(q):
    return slice(128 * q, 128 * q + 128)


def splat(table_ref, d, field):
    return table_ref[pl.ds(d * FIELDS + field, 8, stride=0), :]


def form_moments(dates, load, w_ref, table_ref, s_ref, out_ref):
    masks = flip_masks()
    zero = jnp.zeros((8, 128), F32)

    def put(row, q, v):
        out_ref[pl.ds(q * 8 * DEEP + row, 8, stride=DEEP), :] = flip(v, masks)

    for b in range(BANDS):

        def body(d, carry):
            acc, square = list(carry[0]), list(carry[1])
            wy = []
            for q in range(TILES):
                y = load(b, d, q)
                v = w_ref[d, :, tile(q)] * y
                square[q] = square[q] + v * y
                wy.append(v)
            for k in range(TERMS):
                x = splat(table_ref, d, COLUMN[k])
                for q in range(TILES):
                    acc[k * TILES + q] = acc[k * TILES + q] + x * wy[q]
            return tuple(acc), tuple(square)

        acc, square = lax.fori_loop(
            0, dates, body, ((zero,) * (TERMS * TILES), (zero,) * TILES)
        )
        for k in range(TERMS):
            for q in range(TILES):
                put(8 * k + b, q, acc[k * TILES + q])
        for q in range(TILES):
            if b == 0:
                s_ref[:, tile(q)] = square[q]
            else:
                s_ref[:, tile(q)] = s_ref[:, tile(q)] + square[q]
    for first in range(0, EXTRA_S, 7):
        fields = list(range(first, min(first + 7, EXTRA_S)))

        def body(d, acc):
            acc = list(acc)
            w = [w_ref[d, :, tile(q)] for q in range(TILES)]
            for n, e in enumerate(fields):
                if e == 0:
                    for q in range(TILES):
                        acc[q] = acc[q] + w[q]
                    continue
                x = splat(table_ref, d, e)
                for q in range(TILES):
                    acc[n * TILES + q] = acc[n * TILES + q] + x * w[q]
            return tuple(acc)

        acc = lax.fori_loop(0, dates, body, (zero,) * (len(fields) * TILES))
        for n, e in enumerate(fields):
            for q in range(TILES):
                put(extra_row(e), q, acc[n * TILES + q])
    for q in range(TILES):
        put(extra_row(EXTRA_S), q, s_ref[:, tile(q)])
        for row in range(extra_row(EXTRA_S) + 1, DEEP):
            out_ref[pl.ds(q * 8 * DEEP + row, 8, stride=DEEP), :] = zero


def first_kernel(dates, obs_ref, valid_ref, table_ref, out_ref, w_ref, s_ref):
    @pl.loop(0, dates)
    def _(d):
        w_ref[d] = valid_ref[d].astype(F32)

    form_moments(
        dates, lambda b, d, q: obs_ref[b, d, :, tile(q)].astype(F32), w_ref, table_ref, s_ref, out_ref
    )


def second_kernel(
    dates, obs_ref, valid_ref, table_ref, block_ref, out_ref, beta_ref, r_ref, w_ref, s_ref
):
    masks = flip_masks()

    def get(row, q):
        return flip(block_ref[pl.ds(q * 8 * BLOCK + row, 8, stride=BLOCK), :], masks)

    for b in range(BANDS):
        beta = [[get(8 * k + b, q) for q in range(TILES)] for k in range(TERMS)]

        def body(d, carry):
            x = [splat(table_ref, d, COLUMN[k]) for k in range(TERMS)]
            for q in range(TILES):
                fit = beta[0][q]
                for k in range(1, TERMS):
                    fit = fit + x[k] * beta[k][q]
                r = obs_ref[b, d, :, tile(q)].astype(F32) - fit
                r_ref[b, d, :, tile(q)] = r
                if b == 0:
                    w_ref[d, :, tile(q)] = r * r
                else:
                    w_ref[d, :, tile(q)] = w_ref[d, :, tile(q)] + r * r
            return carry

        lax.fori_loop(0, dates, body, 0)
    scale = [1.0 / (float(BANDS) * (TUKEY * TUKEY) * (get(7, q) + EPS)) for q in range(TILES)]

    @pl.loop(0, dates)
    def _(d):
        for q in range(TILES):
            left = 1.0 - jnp.minimum(w_ref[d, :, tile(q)] * scale[q], 1.0)
            w_ref[d, :, tile(q)] = valid_ref[d, :, tile(q)].astype(F32) * left * left

    form_moments(
        dates, lambda b, d, q: r_ref[b, d, :, tile(q)], w_ref, table_ref, s_ref, out_ref
    )


def copy_to(src, dst, send, recv, space, date):
    return pltpu.make_async_remote_copy(
        src_ref=src, dst_ref=dst, send_sem=send, recv_sem=recv, device_id=(space, date), device_id_type=MESH
    )


def place():
    s, j = lax.axis_index("space"), lax.axis_index("date")
    return s, j, j // ZS, lax.rem(j, ZS)


def wrap(value, count):
    return lax.rem(value + count, count)


def barrier():
    s, j, x, z = place()
    sem = pltpu.get_barrier_semaphore()
    targets = [(s, x * ZS + wrap(z + 1, ZS)), (s, x * ZS + wrap(z - 1, ZS)), (s, (1 - x) * ZS + z)]
    targets += [(wrap(s + a, 16), wrap(j + b, SHARDS)) for a, b in NEIGHBOURS]
    for target in targets:
        pl.semaphore_signal(sem, inc=1, device_id=target, device_id_type=MESH)
    pl.semaphore_wait(sem, len(targets))


def reduce_scatter(mom_ref, slot_ref, mine_ref, other_ref, landed_ref, sems):
    ring_send, ring_recv, x_send, x_recv = sems
    s, j, x, z = place()
    to = [(s, x * ZS + wrap(z + 1, ZS)), (s, x * ZS + wrap(z - 1, ZS))]
    side = [1 - x, 1 - x, x, x]

    def rows(shard_z, ch):
        start = (side[ch] * ZS + shard_z) * DEEP + HALF * (ch % 2)
        return pl.ds(pl.multiple_of(start, 8), HALF)

    def target(way, step):
        return wrap(z + 8 - step, ZS) if way == 0 else wrap(z - 7 + step, ZS)

    def hop(way, step, ch, src):
        return copy_to(
            src, slot_ref.at[way, step, ch], ring_send.at[way, step, ch], ring_recv.at[way, step, ch], *to[way]
        )

    for ch in range(4):
        for way in range(2):
            hop(way, 0, ch, mom_ref.at[rows(target(way, 0), ch)]).start()

    def add(way, step, ch):
        hop(way, step - 1, ch, slot_ref.at[way, step - 1, ch]).wait_recv()
        slot_ref[way, step - 1, ch] = slot_ref[way, step - 1, ch] + mom_ref[rows(target(way, step), ch), :]
        hop(way, step, ch, slot_ref.at[way, step - 1, ch]).start()

    def body(step, carry):
        for ch in range(4):
            add(0, step, ch)
            add(1, step, ch)
        return carry

    lax.fori_loop(1, 7, body, 0)
    for ch in range(4):
        add(0, 7, ch)
    swaps = []
    for ch in range(4):
        hop(0, 7, ch, slot_ref.at[0, 7, ch]).wait_recv()
        hop(1, 6, ch, slot_ref.at[1, 6, ch]).wait_recv()
        total = mom_ref[rows(z, ch), :] + slot_ref[0, 7, ch] + slot_ref[1, 6, ch]
        if ch < 2:
            other_ref[ch] = total
            swap = copy_to(
                other_ref.at[ch], landed_ref.at[ch], x_send.at[ch], x_recv.at[ch], s, (1 - x) * ZS + z
            )
            swap.start()
            swaps.append(swap)
        else:
            h = ch - 2
            swaps[h].wait_recv()
            mine_ref[HALF * h : HALF * h + HALF, :] = total + landed_ref[h]
    for swap in swaps:
        swap.wait_send()

    def drain(step, carry):
        for ch in range(4):
            hop(0, step, ch, slot_ref.at[0, step, ch]).wait_send()
            hop(1, step, ch, slot_ref.at[1, step, ch]).wait_send()
        return carry

    lax.fori_loop(0, 7, drain, 0)
    for ch in range(4):
        hop(0, 7, ch, slot_ref.at[0, 7, ch]).wait_send()


def solve(mine_ref, base):
    moment = {}

    def mom(e):
        if e not in moment:
            moment[e] = jnp.broadcast_to(mine_ref[extra_row(e) : extra_row(e) + 1, :], (8, 128))
        return moment[e]

    gram = {}
    for i in range(TERMS):
        for j in range(i, TERMS):
            value = None
            for factor, e in gram_terms(i, j):
                part = mom(e) if factor == 1.0 else factor * mom(e)
                value = part if value is None else value + part
            gram[i, j] = value
    cross = [mine_ref[8 * k : 8 * k + 8, :] for k in range(TERMS)]
    work = dict(gram)
    for i in range(TERMS):
        work[i, i] = work[i, i] + 1.0
    right = [cross[k] if base is None else cross[k] - base[k] for k in range(TERMS)]
    inverse, factor = [], {}
    for i in range(TERMS):
        inv = 1.0 / work[i, i]
        inverse.append(inv)
        for r in range(i + 1, TERMS):
            factor[r, i] = work[i, r] * inv
        for r in range(i + 1, TERMS):
            for c in range(r, TERMS):
                work[r, c] = work[r, c] - factor[r, i] * work[i, c]
            right[r] = right[r] - factor[r, i] * right[i]
    answer = [None] * TERMS
    for i in reversed(range(TERMS)):
        value = right[i] * inverse[i]
        for c in range(i + 1, TERMS):
            value = value - factor[c, i] * answer[c]
        answer[i] = value
    lost = None
    for i in range(TERMS):
        image = None
        for c in range(TERMS):
            part = gram[min(i, c), max(i, c)] * answer[c]
            image = part if image is None else image + part
        part = answer[i] * (2.0 * cross[i] - image)
        lost = part if lost is None else lost + part
    sub = lax.broadcasted_iota(jnp.int32, (8, 128), 0)
    lost = jnp.sum(jnp.where(sub < BANDS, lost, 0.0), axis=0, keepdims=True)
    spread = jnp.maximum(mom(EXTRA_S) - jnp.broadcast_to(lost, (8, 128)), 0.0) * (1.0 / BANDS)
    return answer, spread / (1.0 + mom(0))


def swap_halo(variance, own_ref, near_ref, sems):
    send, recv = sems
    s, j, x, z = place()
    own_ref[...] = variance
    copies = []
    for n, (a, b) in enumerate(NEIGHBOURS):
        back = NEIGHBOURS.index((-a, -b))
        copy = copy_to(
            own_ref, near_ref.at[back], send.at[n], recv.at[back], wrap(s + a, 16), wrap(j + b, SHARDS)
        )
        copy.start()
        copies.append(copy)
    return copies


def box_mean(variance, near_ref, copies):
    s, j, x, z = place()
    for copy in copies:
        copy.wait()
    lane = lax.broadcasted_iota(jnp.int32, (8, 128), 1)
    col, row = lane % 16, lane // 16

    def field(a, b):
        if (a, b) == (0, 0):
            return variance
        value = near_ref[NEIGHBOURS.index((a, b))]
        inside = jnp.int32(1)
        if a:
            inside = inside * ((s + a >= 0) & (s + a < 16)).astype(jnp.int32)
        if b:
            inside = inside * ((j + b >= 0) & (j + b < SHARDS)).astype(jnp.int32)
        return jnp.where(jnp.full((8, 128), inside) > 0, value, 0.0)

    across = []
    for a in (-1, 0, 1):
        middle = field(a, 0)
        left = pltpu.roll(field(a, -1), 128 - 16, 1)
        right = pltpu.roll(field(a, 1), 16, 1)
        total = middle
        for step in (1, 2):
            total = total + pltpu.roll(jnp.where(col < step, right, middle), 128 - step, 1)
            total = total + pltpu.roll(jnp.where(col >= 16 - step, left, middle), step, 1)
        across.append(total)
    up, middle, down = across
    total = middle
    for step in (1, 2):
        total = total + pltpu.roll(jnp.where(row < step, down, middle), 128 - 16 * step, 1)
        total = total + pltpu.roll(jnp.where(row >= 8 - step, up, middle), 16 * step, 1)

    def count(index, whole):
        return (jnp.minimum(index + 2, whole - 1) - jnp.maximum(index - 2, 0) + 1).astype(F32)

    return total / (count(s * 8 + row, 128) * count(j * 16 + col, COLS))


def first_exchange(
    mom_ref, out_ref, slot_ref, mine_ref, other_ref, landed_ref, own_ref, near_ref,
    ring_send, ring_recv, x_send, x_recv, h_send, h_recv, g_send, g_recv, gx_send, gx_recv,
):
    s, j, x, z = place()
    barrier()
    reduce_scatter(mom_ref, slot_ref, mine_ref, other_ref, landed_ref, (ring_send, ring_recv, x_send, x_recv))
    answer, variance = solve(mine_ref, None)
    copies = swap_halo(variance, own_ref, near_ref, (h_send, h_recv))
    to = [(s, x * ZS + wrap(z + 1, ZS)), (s, x * ZS + wrap(z - 1, ZS))]
    side = [x, x, 1 - x, 1 - x]
    size = BLOCK // 2

    def part(owner_z, ch):
        start = (side[ch] * ZS + owner_z) * BLOCK + size * (1 - ch % 2)
        return out_ref.at[pl.ds(pl.multiple_of(start, 8), size)]

    def owner(way, step):
        return wrap(z - step, ZS) if way == 0 else wrap(z + step, ZS)

    def hop(way, step, ch):
        piece = part(owner(way, step), ch)
        return copy_to(piece, piece, g_send.at[way, step, ch], g_recv.at[way, step, ch], *to[way])

    def arrived(way, step, ch):
        piece = part(owner(way, step + 1), ch)
        copy_to(piece, piece, g_send.at[way, step, ch], g_recv.at[way, step, ch], *to[way]).wait_recv()

    def cross(ch, source):
        start = (source * ZS + z) * BLOCK + size * (1 - ch % 2)
        piece = out_ref.at[pl.ds(pl.multiple_of(start, 8), size)]
        return copy_to(piece, piece, gx_send.at[ch], gx_recv.at[ch], s, (1 - x) * ZS + z)

    sub = lax.broadcasted_iota(jnp.int32, (8, 128), 0)
    base = j * BLOCK
    for k in range(4, TERMS):
        out_ref[pl.ds(pl.multiple_of(base + 8 * k, 8), 8), :] = jnp.where(sub < BANDS, answer[k], 0.0)
    cross(0, x).start()
    for way in range(2):
        hop(way, 0, 0).start()
    smooth = box_mean(variance, near_ref, copies)
    for k in range(4):
        out_ref[pl.ds(pl.multiple_of(base + 8 * k, 8), 8), :] = jnp.where(sub < BANDS, answer[k], smooth)
    cross(1, x).start()
    for way in range(2):
        hop(way, 0, 1).start()
    for ch in range(2):
        cross(ch, 1 - x).wait_recv()
        for way in range(2):
            hop(way, 0, 2 + ch).start()

    def body(step, carry):
        for ch in range(4):
            for way in range(2):
                arrived(way, step - 1, ch)
                hop(way, step, ch).start()
        return carry

    lax.fori_loop(1, 7, body, 0)
    for ch in range(4):
        arrived(0, 6, ch)
        hop(0, 7, ch).start()
    for ch in range(4):
        arrived(1, 6, ch)
    for ch in range(4):
        arrived(0, 7, ch)
    for ch in range(2):
        cross(ch, x).wait_send()

    def drain(step, carry):
        for ch in range(4):
            for way in range(2):
                hop(way, step, ch).wait_send()
        return carry

    lax.fori_loop(0, 7, drain, 0)
    for ch in range(4):
        hop(0, 7, ch).wait_send()


def second_exchange(
    mom_ref, block_ref, coef_ref, noise_ref, slot_ref, mine_ref, other_ref, landed_ref, own_ref, near_ref,
    ring_send, ring_recv, x_send, x_recv, h_send, h_recv,
):
    s, j, x, z = place()
    barrier()
    reduce_scatter(mom_ref, slot_ref, mine_ref, other_ref, landed_ref, (ring_send, ring_recv, x_send, x_recv))
    base = [block_ref[pl.ds(pl.multiple_of(j * BLOCK + 8 * k, 8), 8), :] for k in range(TERMS)]
    answer, variance = solve(mine_ref, base)
    copies = swap_halo(variance, own_ref, near_ref, (h_send, h_recv))
    masks = flip_masks()
    for k in range(TERMS):
        spread = flip(base[k] + answer[k], masks)
        for b in range(BANDS):
            turned = spread if b == 0 else pltpu.roll(spread, 128 - 16 * b, 1)
            coef_ref[b, k] = turned[:, :16]
    smooth = box_mean(variance, near_ref, copies)
    noise_ref[...] = flip(jnp.sqrt(smooth + EPS), masks)[:, :16]


def exchange_scratch():
    ring = pltpu.SemaphoreType.DMA((2, 8, 4))
    two, eight = pltpu.SemaphoreType.DMA((2,)), pltpu.SemaphoreType.DMA((8,))
    return [
        pltpu.VMEM((2, 8, 4, HALF, 128), F32),
        pltpu.VMEM((DEEP, 128), F32),
        pltpu.VMEM((2, HALF, 128), F32),
        pltpu.VMEM((2, HALF, 128), F32),
        pltpu.VMEM((8, 128), F32),
        pltpu.VMEM((8, 8, 128), F32),
        ring, ring, two, two, eight, eight,
    ]


def vmem(count):
    return [pl.BlockSpec(memory_space=pltpu.VMEM)] * count


def on_device(obs, valid, days):
    dates = obs.shape[1]
    table = design_table(days)
    moments = jax.ShapeDtypeStruct((SHARDS * DEEP, 128), F32)
    weights = pltpu.VMEM((dates, ROWS, COLS), F32)
    squares = pltpu.VMEM((ROWS, COLS), F32)
    params = pltpu.CompilerParams(vmem_limit_bytes=48 << 20)
    first = pl.pallas_call(
        functools.partial(first_kernel, dates),
        out_shape=moments,
        in_specs=vmem(3),
        out_specs=vmem(1)[0],
        scratch_shapes=[weights, squares],
        compiler_params=params,
    )(obs, valid, table)
    ring = pltpu.SemaphoreType.DMA((2, 8, 4))
    two = pltpu.SemaphoreType.DMA((2,))
    block = pl.pallas_call(
        first_exchange,
        out_shape=jax.ShapeDtypeStruct((SHARDS * BLOCK, 128), F32),
        in_specs=vmem(1),
        out_specs=vmem(1)[0],
        scratch_shapes=exchange_scratch() + [ring, ring, two, two],
        compiler_params=pltpu.CompilerParams(collective_id=0, has_side_effects=True, vmem_limit_bytes=48 << 20),
    )(first)
    second = pl.pallas_call(
        functools.partial(second_kernel, dates),
        out_shape=moments,
        in_specs=vmem(4),
        out_specs=vmem(1)[0],
        scratch_shapes=[
            pltpu.VMEM((BANDS * TERMS, ROWS, 128), F32),
            pltpu.VMEM((BANDS, dates, ROWS, COLS), F32),
            weights,
            squares,
        ],
        compiler_params=params,
    )(obs, valid, table, block)
    return pl.pallas_call(
        second_exchange,
        out_shape=(
            jax.ShapeDtypeStruct((BANDS, TERMS, ROWS, 16), F32),
            jax.ShapeDtypeStruct((ROWS, 16), F32),
        ),
        in_specs=vmem(2),
        out_specs=tuple(vmem(2)),
        scratch_shapes=exchange_scratch(),
        compiler_params=pltpu.CompilerParams(collective_id=1, has_side_effects=True, vmem_limit_bytes=48 << 20),
    )(second, block)


def solution(mesh):
    in_specs = (P(None, "date", "space", None), P("date", "space", None), P("date"))
    out_specs = (P(None, None, "space", "date"), P("space", "date"))
    return jax.shard_map(on_device, mesh=mesh, in_specs=in_specs, out_specs=out_specs, check_vma=False)
```

time: 879 us -> 140 us (0.16)
  waiting for transfers between devices: 482 us -> 0 us
  blocking collectives: 187 us -> 0 us
  Pallas kernels: 0 us -> 133 us
  starting transfers between devices: 113 us -> 0 us
  other arithmetic: 46.9 us -> 0.72 us
  local copies, waits for them, and re-layouts: 20.9 us -> 5.69 us
  between operations: 14.6 us -> 0.72 us
  matrix products: 12 us -> 0 us
    psum x2 -> x0, waiting for transfers between devices: 477 us -> none  [on_device(): summed = lax.psum(local_terms, 'date')]
    psum x2 -> x0, blocking collectives: 187 us -> none  [spread_rows(): full_spread = lax.psum(spread, 'date')]
    pallas_call x0 -> x4, Pallas kernels: none -> 133 us  [the longest x1 70.8 us: on_device(): pl.pallas_call(first_exchange, out_shape=jax.ShapeDtypeStruct((SHARDS * B...]
    ppermute x4 -> x0, starting transfers between devices: 113 us -> none  [the longest x2 109 us: padded_2(): lax.ppermute(lax.slice_in_dim(block, block.shape[dim] - width, None, axis...]
    div x20 -> x0, other arithmetic: 24.5 us -> none  [the longest x9 17.5 us: solve_terms(): solved[row_index] = running / lower_factor[row_index, row_index][None]]
    dot_general x6 -> x0, matrix products: 12 us -> none  [the longest x2 7.52 us: residual_power(): jnp.einsum('dk,bkp->bdp', design_rows, coefficient, precision=highest, pr...]
    sqrt x13 -> x0, other arithmetic: 9.05 us -> none  [the longest x12 7.69 us: solve_terms(): pivot_root = jnp.sqrt(pivot_value)]
  transfers between devices with their start and end apart: 6 -> 0, of which waited for: 4 -> 0; matrix products, arithmetic and copies ran while one was open for 0% -> 0% of each run, Pallas kernels for 0% -> 0%
where the time goes in v1:
time: 140 us
  Pallas kernels  133 us (95%)
  local copies, waits for them, and re-layouts  5.69 us (4%)
    pallas_call x1, Pallas kernels, on_device(): pl.pallas_call(first_exchange, out_shape=jax.ShapeDtypeStruct((SHARDS * B...  70.8 us
    pallas_call x1, Pallas kernels, on_device(): pl.pallas_call(second_exchange, out_shape=(jax.ShapeDtypeStruct((BANDS, T...  40.9 us
    pallas_call x1, Pallas kernels, on_device(): pl.pallas_call(functools.partial(second_kernel, dates), out_shape=moments...  13.2 us
    pallas_call x1, Pallas kernels, on_device(): pl.pallas_call(functools.partial(first_kernel, dates), out_shape=moments,...  8.05 us
    unnamed x8, local copies, waits for them, and re-layouts  3.62 us

profile of v1, /device:TPU:1, one launch (start us, length us, event | category | flops | bytes accessed | tf_op | source)
XLA Modules:
  0.0 140.1 jit_solution(16284697844181848066)
XLA Ops:
  0.6 0.7 multiply_bitcast_fusion
  1.4 0.1 copy.24
  1.4 0.1 copy.6
  1.5 0.1 copy.20
  1.6 0.1 copy.10
  1.7 0.1 copy.21
  1.8 0.1 copy.12
  1.9 0.1 copy.16
  1.9 0.1 copy.23
  2.0 0.1 copy.15
  2.1 0.1 copy.17
  2.2 0.1 copy.18
  2.3 0.1 copy.22
  2.4 0.1 copy.19
  2.5 0.1 copy.11
  2.5 0.1 copy.14
  2.6 0.1 copy.13
  2.7 0.1 copy.7
  2.8 0.1 copy.8
  2.9 0.1 copy.9
  3.0 0.1 copy.5
  3.1 0.1 stack.87
  3.2 0.1 broadcast_in_dim.7
  3.3 0.1 broadcast_in_dim.8.table_ref
  3.5 0.0 copy-start
  3.5 1.3 copy-done
  4.8 0.0 copy-start.2
  4.8 1.0 copy-done.2
  5.8 8.1 %shard_map.50.mom_ref = f32[2560,128]{1,0:T(8,128)S(1)} custom-call(bf16[7,24,8,512]{3,2,1,0:T(8,128)(2,1)S(1)} %copy-done, s32[24,8,512]{2,1,0:T(8,128)S(1)} %copy-done.2, f32[576,128]{1,0:T(8,128)S(1)} %broadcast_in_dim.8.table_ref), custom_call_target="tpu_custom_call" | custom-call | tf_op jit(solution)/shard_map/pallas_call | solution.py:542
  13.9 0.0 copy-start.1
  13.9 70.8 %shard_map.51.block_ref = f32[2048,128]{1,0:T(8,128)S(1)} custom-call(f32[2560,128]{1,0:T(8,128)S(1)} %shard_map.50.mom_ref), custom_call_target="tpu_custom_call" | custom-call | tf_op jit(solution)/shard_map/pallas_call | solution.py:552
  84.6 0.0 copy-done.1
  84.6 13.2 %shard_map.52.mom_ref = f32[2560,128]{1,0:T(8,128)S(1)} custom-call(bf16[7,24,8,512]{3,2,1,0:T(8,128)(2,1)S(1)} %copy-done.1, s32[24,8,512]{2,1,0:T(8,128)S(1)} %copy-done.2, f32[576,128]{1,0:T(8,128)S(1)} %broadcast_in_dim.8.table_ref, f32[2048,128]{1,0:T(8,128)S(1)} %shard_map.51.block_ref), custom_call_target="tpu_custom_call" | custom-call | tf_op jit(solution)/shard_map/pallas_call | solution.py:560
  97.9 40.9 %shard_map.53 = (f32[7,8,8,16]{3,2,1,0:T(8,128)S(1)}, f32[8,16]{1,0:T(8,128)S(1)}) custom-call(f32[2560,128]{1,0:T(8,128)S(1)} %shard_map.52.mom_ref, f32[2048,128]{1,0:T(8,128)S(1)} %shard_map.51.block_ref), custom_call_target="tpu_custom_call" | custom-call | tf_op jit(solution)/shard_map/pallas_call | solution.py:573
  138.8 0.7 copy.27
  139.5 0.6 copy.28
  (3 shorter events, 0.0 us)
Async XLA Ops:
  3.5 1.3 copy-start
  4.8 1.0 copy-start.2
  13.9 70.8 %copy-start.1 = (bf16[7,24,8,512]{3,2,1,0:T(8,128)(2,1)S(1)}, bf16[7,24,8,512]{3,2,1,0:T(8,128)(2,1)}, u32[]{:S(2)}) copy-start(bf16[7,24,8,512]{3,2,1,0:T(8,128)(2,1)} %obs_ref.3) | copy-start | bytes 4128772

commit v2 on v1

v2 whole, which is shorter than its diff:
```python
import functools
import math

import jax
import jax.numpy as jnp
from jax import lax
from jax.experimental import pallas as pl
from jax.experimental.pallas import tpu as pltpu
from jax.sharding import PartitionSpec as P

F32 = jnp.float32
MESH = pl.DeviceIdType.MESH
TUKEY = 4.685
EPS = 1e-06
BANDS = 7
TERMS = 8
ROWS = 8
COLS = 512
TILES = 4
SHARDS = 32
DEEP = 80
BLOCK = 64
FIELDS = 24
ZS = 16

C0, S0, TC0, TS0, EXTRA_S = 2, 8, 14, 17, 21
NEIGHBOURS = [(a, b) for a in (-1, 0, 1) for b in (-1, 0, 1) if (a, b) != (0, 0)]


PIECES = ((0, 16), (16, 24), (40, 16), (56, 24))
CHAINS = ((1, 8), (1, 7), (-1, 7), (-1, 6))
SPREADS = ((1, 2, 4), (1, 1, 4), (-1, 1, 4), (-1, 2, 3))
PARTS = ((0, 32), (32, 24), (56, 8))


def extra_row(e):
    return 8 * BANDS + e


def gram_terms(i, j):
    if i > j:
        i, j = j, i
    if i == 0:
        if j < 2:
            return [(1.0, j)]
        n = j // 2
        return [(1.0, (C0 if j % 2 == 0 else S0) + n)]
    if i == 1:
        if j == 1:
            return [(1.0, 2)]
        n = j // 2
        return [(1.0, (TC0 if j % 2 == 0 else TS0) + n)]
    a, b = i // 2, j // 2

    def cosine(n):
        return 0 if n == 0 else C0 + n

    if i % 2 == 0 and j % 2 == 0:
        return [(0.5, cosine(abs(a - b))), (0.5, cosine(a + b))]
    if i % 2 == 1 and j % 2 == 1:
        return [(0.5, cosine(abs(a - b))), (-0.5, cosine(a + b))]
    s, c = (a, b) if i % 2 == 1 else (b, a)
    terms = [(0.5, S0 + s + c)]
    if s != c:
        terms.append((0.5 if s > c else -0.5, S0 + abs(s - c)))
    return terms


def design_table(dates, days_ref, table_ref):
    rows = lax.broadcasted_iota(jnp.int32, (dates, 128), 0)
    day = jnp.zeros((dates, 128), F32)
    for d in range(dates):
        day = jnp.where(rows == d, days_ref[d].astype(F32), day)
    angle = day * (2.0 * math.pi / 365.25)
    t = (day - 1825.0) / 1825.0
    c = [None] + [jnp.cos(h * angle) for h in range(1, 4)]
    s = [None] + [jnp.sin(h * angle) for h in range(1, 4)]
    c += [2 * c[2] * c[2] - 1, c[2] * c[3] - s[2] * s[3], 2 * c[3] * c[3] - 1]
    s += [2 * s[2] * c[2], s[2] * c[3] + c[2] * s[3], 2 * s[3] * c[3]]
    fields = [jnp.ones_like(t), t, t * t] + c[1:] + s[1:]
    fields += [t * c[h] for h in range(1, 4)] + [t * s[h] for h in range(1, 4)]
    for f, value in enumerate(fields):
        for first in range(0, dates, 8):
            table_ref[pl.ds(first * FIELDS + f, 8, stride=FIELDS), :] = value[first : first + 8]


COLUMN = [0, 1, C0 + 1, S0 + 1, C0 + 2, S0 + 2, C0 + 3, S0 + 3]


def flip_masks():
    sub = lax.broadcasted_iota(jnp.int32, (8, 128), 0)
    group = lax.broadcasted_iota(jnp.int32, (8, 128), 1) // 16
    masks = []
    for bit in (4, 2, 1):
        s, g = (sub & bit) != 0, (group & bit) != 0
        masks.append((jnp.logical_and(s, jnp.logical_not(g)), jnp.logical_and(jnp.logical_not(s), g)))
    return masks


def flip(v, masks):
    for bit, (low, high) in zip((4, 2, 1), masks):
        up = pltpu.roll(pltpu.roll(v, bit, 0), 128 - 16 * bit, 1)
        if bit == 4:
            v = jnp.where(jnp.logical_or(low, high), up, v)
        else:
            down = pltpu.roll(pltpu.roll(v, 8 - bit, 0), 16 * bit, 1)
            v = jnp.where(low, up, jnp.where(high, down, v))
    return v


def tile(q):
    return slice(128 * q, 128 * q + 128)


def splat(table_ref, d, field):
    return table_ref[pl.ds(d * FIELDS + field, 8, stride=0), :]


def form_moments(dates, load, w_ref, table_ref, s_ref, out_refs, ready, done):
    masks = flip_masks()
    zero = jnp.zeros((8, 128), F32)

    def put(row, q, v):
        for (first, count), out_ref in zip(PIECES, out_refs):
            if first <= row < first + count:
                out_ref[pl.ds(q * 8 * count + row - first, 8, stride=count), :] = v

    def finish(row):
        for n, (first, count) in enumerate(PIECES):
            if row == first + count:
                done(n)

    for b in range(BANDS):
        ready(b)

        def body(d, carry):
            acc, square = list(carry[0]), list(carry[1])
            wy = []
            for q in range(TILES):
                y = load(b, d, q)
                v = w_ref[d, :, tile(q)] * y
                square[q] = square[q] + v * y
                wy.append(v)
            for k in range(TERMS):
                x = splat(table_ref, d, COLUMN[k]) if k else None
                for q in range(TILES):
                    acc[k * TILES + q] = acc[k * TILES + q] + (x * wy[q] if k else wy[q])
            return tuple(acc), tuple(square)

        acc, square = lax.fori_loop(
            0, dates, body, ((zero,) * (TERMS * TILES), (zero,) * TILES)
        )
        for k in range(TERMS):
            for q in range(TILES):
                put(8 * b + k, q, flip(acc[k * TILES + q], masks))
        for q in range(TILES):
            if b == 0:
                s_ref[:, tile(q)] = square[q]
            else:
                s_ref[:, tile(q)] = s_ref[:, tile(q)] + square[q]
        finish(8 * b + 8)
    for first in range(0, EXTRA_S, 7):
        fields = list(range(first, min(first + 7, EXTRA_S)))

        def body(d, acc):
            acc = list(acc)
            w = [w_ref[d, :, tile(q)] for q in range(TILES)]
            for n, e in enumerate(fields):
                x = splat(table_ref, d, e) if e else None
                for q in range(TILES):
                    acc[n * TILES + q] = acc[n * TILES + q] + (x * w[q] if e else w[q])
            return tuple(acc)

        acc = lax.fori_loop(0, dates, body, (zero,) * (len(fields) * TILES))
        for n, e in enumerate(fields):
            for q in range(TILES):
                put(extra_row(e), q, flip(acc[n * TILES + q], masks))
    for q in range(TILES):
        put(extra_row(EXTRA_S), q, flip(s_ref[:, tile(q)], masks))
        for row in range(extra_row(EXTRA_S) + 1, DEEP):
            put(row, q, zero)
    finish(DEEP)


def form_residuals(dates, obs_ref, valid_ref, table_ref, block_ref, r_ref, w_ref):
    masks = flip_masks()

    def get(row, q):
        return flip(block_ref[pl.ds(q * 8 * BLOCK + row, 8, stride=BLOCK), :], masks)

    for b in range(BANDS):
        beta = [[get(8 * b + k, q) for q in range(TILES)] for k in range(TERMS)]

        def body(d, carry):
            x = [splat(table_ref, d, COLUMN[k]) if k else None for k in range(TERMS)]
            for q in range(TILES):
                fit = beta[0][q]
                for k in range(1, TERMS):
                    fit = fit + x[k] * beta[k][q]
                r = obs_ref[b, d, :, tile(q)].astype(F32) - fit
                r_ref[b, d, :, tile(q)] = r
                if b == 0:
                    w_ref[d, :, tile(q)] = r * r
                else:
                    w_ref[d, :, tile(q)] = w_ref[d, :, tile(q)] + r * r
            return carry

        lax.fori_loop(0, dates, body, 0)
    scale = [1.0 / (float(BANDS) * (TUKEY * TUKEY) * (get(8 * BANDS, q) + EPS)) for q in range(TILES)]

    @pl.loop(0, dates)
    def _(d):
        for q in range(TILES):
            left = 1.0 - jnp.minimum(w_ref[d, :, tile(q)] * scale[q], 1.0)
            w_ref[d, :, tile(q)] = valid_ref[d, :, tile(q)].astype(F32) * left * left


def copy_to(src, dst, send, recv, space, date):
    return pltpu.make_async_remote_copy(
        src_ref=src, dst_ref=dst, send_sem=send, recv_sem=recv, device_id=(space, date), device_id_type=MESH
    )


def place():
    s, j = lax.axis_index("space"), lax.axis_index("date")
    return s, j, j // ZS, lax.rem(j, ZS)


def wrap(value, count):
    return lax.rem(value + count, count)


def greet():
    s, j, x, z = place()
    sem = pltpu.get_barrier_semaphore()
    targets = [(s, x * ZS + wrap(z + h, ZS)) for h in (1, -1, 2, -2)] + [(s, (1 - x) * ZS + z)]
    targets += [(wrap(s + a, 16), wrap(j + b, SHARDS)) for a, b in NEIGHBOURS]
    for target in targets:
        pl.semaphore_signal(sem, inc=1, device_id=target, device_id_type=MESH)
    return sem, len(targets)


class Reduction:
    def __init__(self, mom_refs, land_refs, slot_ref, mine_ref, sems):
        self.mom, self.land, self.slot, self.mine = mom_refs, land_refs, slot_ref, mine_ref
        self.x_send, self.x_recv, self.send, self.recv = sems
        self.s, self.j, self.x, self.z = place()

    def swap(self, n):
        size = ZS * PIECES[n][1]
        other = pl.multiple_of((1 - self.x) * size, 8)
        return copy_to(
            self.mom[n].at[pl.ds(other, size)], self.land[n], self.x_send.at[n], self.x_recv.at[n],
            self.s, (1 - self.x) * ZS + self.z,
        )

    def landed(self, n):
        self.swap(n).wait_recv()
        size = ZS * PIECES[n][1]
        own = pl.multiple_of(self.x * size, 8)
        self.land[n][...] = self.land[n][...] + self.mom[n][pl.ds(own, size), :]

    def length(self, chain):
        return (CHAINS[chain][1] + 1) // 2

    def rows(self, n, chain, step):
        way, first = CHAINS[chain]
        count = PIECES[n][1]
        return pl.ds(pl.multiple_of(wrap(self.z + way * (first - 2 * step), ZS) * count, 8), count)

    def place_of(self, n, chain, step):
        return self.slot.at[chain, step, pl.ds(*PIECES[n])]

    def hop(self, n, chain, step):
        way, first = CHAINS[chain]
        reach = min(2, first - 2 * step)
        source = self.land[n].at[self.rows(n, chain, 0)] if step == 0 else self.place_of(n, chain, step - 1)
        return copy_to(
            source, self.place_of(n, chain, step), self.send.at[chain, step, n], self.recv.at[chain, step, n],
            self.s, self.x * ZS + wrap(self.z + way * reach, ZS),
        )

    def step(self, n, step):
        for chain in range(4):
            if step >= self.length(chain):
                continue
            if step:
                self.hop(n, chain, step - 1).wait_recv()
                here = self.place_of(n, chain, step - 1)
                here[...] = here[...] + self.land[n][self.rows(n, chain, step), :]
            self.hop(n, chain, step).start()

    def finish(self, n):
        first, count = PIECES[n]
        total = self.land[n][pl.ds(pl.multiple_of(self.z * count, 8), count), :]
        for chain in range(4):
            last = self.length(chain) - 1
            self.hop(n, chain, last).wait_recv()
            total = total + self.slot[chain, last, pl.ds(first, count), :]
        self.mine[pl.ds(first, count), :] = total

    def run(self):
        count = len(PIECES)
        for wave in range(count + 4):
            for n in range(count):
                step = wave - n
                if step == 0:
                    self.landed(n)
                if 0 <= step < 4:
                    self.step(n, step)
                if step == 4:
                    self.finish(n)

    def drain(self):
        for n in range(len(PIECES)):
            self.swap(n).wait_send()
            for chain in range(4):
                for step in range(self.length(chain)):
                    self.hop(n, chain, step).wait_send()


class Spread:
    def __init__(self, block_ref, sems):
        self.block = block_ref
        self.send, self.recv, self.x_send, self.x_recv, self.own_send, self.own_recv = sems
        self.s, self.j, self.x, self.z = place()

    def piece(self, side, owner, n):
        first, count = PARTS[n]
        start = (side * ZS + wrap(owner + ZS, ZS)) * BLOCK + first
        return self.block.at[pl.ds(pl.multiple_of(start, 8), count)]

    def offset(self, chain, step):
        way, first, _ = SPREADS[chain]
        return 0 if step == 0 else way * (first + 2 * (step - 1))

    def hop(self, n, chain, step):
        way, first, _ = SPREADS[chain]
        reach = first if step == 0 else 2
        piece = self.piece(self.x, self.z - self.offset(chain, step), n)
        return copy_to(
            piece, piece, self.send.at[chain, step, n], self.recv.at[chain, step, n],
            self.s, self.x * ZS + wrap(self.z + way * reach, ZS),
        )

    def arrival(self, n, chain, step):
        piece = self.piece(self.x, self.z - self.offset(chain, step + 1), n)
        return copy_to(
            piece, piece, self.send.at[chain, step, n], self.recv.at[chain, step, n], self.s, self.j
        )

    def across(self, n, chain, step, side):
        piece = self.piece(side, self.z - self.offset(chain, step + 1), n)
        return copy_to(
            piece, piece, self.x_send.at[chain, step, n], self.x_recv.at[chain, step, n],
            self.s, (1 - self.x) * ZS + self.z,
        )

    def own_across(self, n, side):
        piece = self.piece(side, self.z, n)
        return copy_to(
            piece, piece, self.own_send.at[n], self.own_recv.at[n], self.s, (1 - self.x) * ZS + self.z
        )

    def begin(self, n):
        for chain in range(4):
            self.hop(n, chain, 0).start()
        self.own_across(n, self.x).start()

    def relay(self, step):
        for n in range(len(PARTS)):
            for chain in range(4):
                if step <= SPREADS[chain][2]:
                    self.arrival(n, chain, step - 1).wait_recv()
                    if step < SPREADS[chain][2]:
                        self.hop(n, chain, step).start()
                    self.across(n, chain, step - 1, self.x).start()

    def receive(self):
        for n in range(len(PARTS)):
            self.own_across(n, 1 - self.x).wait_recv()
            for chain in range(4):
                for step in range(SPREADS[chain][2]):
                    self.across(n, chain, step, 1 - self.x).wait_recv()

    def drain(self):
        for n in range(len(PARTS)):
            self.own_across(n, self.x).wait_send()
            for chain in range(4):
                for step in range(SPREADS[chain][2]):
                    self.hop(n, chain, step).wait_send()
                    self.across(n, chain, step, self.x).wait_send()


def solve(mine_ref, base):
    moment = {}

    def mom(e):
        if e not in moment:
            moment[e] = jnp.broadcast_to(mine_ref[extra_row(e) : extra_row(e) + 1, :], (8, 128))
        return moment[e]

    gram = {}
    for i in range(TERMS):
        for j in range(i, TERMS):
            value = None
            for factor, e in gram_terms(i, j):
                part = mom(e) if factor == 1.0 else factor * mom(e)
                value = part if value is None else value + part
            gram[i, j] = value
    cross = [mine_ref[pl.ds(k, 8, stride=8), :] for k in range(TERMS)]
    work = dict(gram)
    for i in range(TERMS):
        work[i, i] = work[i, i] + 1.0
    right = [cross[k] if base is None else cross[k] - base[k] for k in range(TERMS)]
    inverse, factor = [], {}
    for i in range(TERMS):
        inv = 1.0 / work[i, i]
        inverse.append(inv)
        for r in range(i + 1, TERMS):
            factor[r, i] = work[i, r] * inv
        for r in range(i + 1, TERMS):
            for c in range(r, TERMS):
                work[r, c] = work[r, c] - factor[r, i] * work[i, c]
            right[r] = right[r] - factor[r, i] * right[i]
    answer = [None] * TERMS
    for i in reversed(range(TERMS)):
        value = right[i] * inverse[i]
        for c in range(i + 1, TERMS):
            value = value - factor[c, i] * answer[c]
        answer[i] = value
    lost = None
    for i in range(TERMS):
        image = None
        for c in range(TERMS):
            part = gram[min(i, c), max(i, c)] * answer[c]
            image = part if image is None else image + part
        part = answer[i] * (2.0 * cross[i] - image)
        lost = part if lost is None else lost + part
    sub = lax.broadcasted_iota(jnp.int32, (8, 128), 0)
    lost = jnp.sum(jnp.where(sub < BANDS, lost, 0.0), axis=0, keepdims=True)
    spread = jnp.maximum(mom(EXTRA_S) - jnp.broadcast_to(lost, (8, 128)), 0.0) * (1.0 / BANDS)
    return answer, spread / (1.0 + mom(0))


def swap_halo(variance, own_ref, near_ref, sems):
    send, recv = sems
    s, j, x, z = place()
    own_ref[...] = variance
    copies = []
    for n, (a, b) in enumerate(NEIGHBOURS):
        back = NEIGHBOURS.index((-a, -b))
        copy = copy_to(
            own_ref, near_ref.at[back], send.at[n], recv.at[back], wrap(s + a, 16), wrap(j + b, SHARDS)
        )
        copy.start()
        copies.append(copy)
    return copies


def box_mean(variance, near_ref, copies):
    s, j, x, z = place()
    for copy in copies:
        copy.wait()
    lane = lax.broadcasted_iota(jnp.int32, (8, 128), 1)
    col, row = lane % 16, lane // 16

    def field(a, b):
        if (a, b) == (0, 0):
            return variance
        value = near_ref[NEIGHBOURS.index((a, b))]
        inside = jnp.int32(1)
        if a:
            inside = inside * ((s + a >= 0) & (s + a < 16)).astype(jnp.int32)
        if b:
            inside = inside * ((j + b >= 0) & (j + b < SHARDS)).astype(jnp.int32)
        return jnp.where(jnp.full((8, 128), inside) > 0, value, 0.0)

    across = []
    for a in (-1, 0, 1):
        middle = field(a, 0)
        left = pltpu.roll(field(a, -1), 128 - 16, 1)
        right = pltpu.roll(field(a, 1), 16, 1)
        total = middle
        for step in (1, 2):
            total = total + pltpu.roll(jnp.where(col < step, right, middle), 128 - step, 1)
            total = total + pltpu.roll(jnp.where(col >= 16 - step, left, middle), step, 1)
        across.append(total)
    up, middle, down = across
    total = middle
    for step in (1, 2):
        total = total + pltpu.roll(jnp.where(row < step, down, middle), 128 - 16 * step, 1)
        total = total + pltpu.roll(jnp.where(row >= 8 - step, up, middle), 16 * step, 1)

    def count(index, whole):
        return (jnp.minimum(index + 2, whole - 1) - jnp.maximum(index - 2, 0) + 1).astype(F32)

    return total / (count(s * 8 + row, 128) * count(j * 16 + col, COLS))


def whole(
    dates, days_ref, obs_hbm, valid_hbm, coef_ref, noise_ref,
    obs_ref, valid_ref, table_ref, w_ref, s_ref, r_ref, block_ref, in_sem, sp0, sp1, sp2, sp3, sp4, sp5, *rest,
):
    s, j, x, z = place()
    valid_copy = pltpu.make_async_copy(valid_hbm, valid_ref, in_sem.at[BANDS])
    valid_copy.start()
    obs_copies = [
        pltpu.make_async_copy(obs_hbm.at[b], obs_ref.at[b], in_sem.at[b]) for b in range(BANDS)
    ]
    for copy in obs_copies:
        copy.start()
    barrier, guests = greet()
    reductions, halos = [], []
    for n in range(2):
        mine_of = rest[18 * n : 18 * n + 18]
        mom, land = mine_of[:4], mine_of[4:8]
        slot, mine, own, near, xs, xr, rs, rr, hs, hr = mine_of[8:]
        reductions.append(Reduction(mom, land, slot, mine, (xs, xr, rs, rr)))
        halos.append((own, near, (hs, hr)))
    design_table(dates, days_ref, table_ref)
    valid_copy.wait()

    @pl.loop(0, dates)
    def _(d):
        w_ref[d] = valid_ref[d].astype(F32)

    red = reductions[0]

    def send_first(n):
        if n == 0:
            pl.semaphore_wait(barrier, guests)
        red.swap(n).start()

    form_moments(
        dates, lambda b, d, q: obs_ref[b, d, :, tile(q)].astype(F32), w_ref, table_ref, s_ref, red.mom,
        lambda b: obs_copies[b].wait(), send_first,
    )
    red.run()
    answer, variance = solve(red.mine, None)
    own_ref, near_ref, halo_sems = halos[0]
    copies = swap_halo(variance, own_ref, near_ref, halo_sems)
    base_row = pl.multiple_of(j * BLOCK, 8)
    for k in range(TERMS):
        block_ref[pl.ds(base_row + k, 8, stride=8), :] = answer[k]
    spread = Spread(block_ref, (sp0, sp1, sp2, sp3, sp4, sp5))
    spread.begin(0)
    spread.begin(1)
    smooth = box_mean(variance, near_ref, copies)
    block_ref[pl.ds(pl.multiple_of(base_row + 8 * BANDS, 8), 8), :] = smooth
    spread.begin(2)
    for step in range(1, 5):
        spread.relay(step)
    red.drain()
    spread.receive()
    form_residuals(dates, obs_ref, valid_ref, table_ref, block_ref, r_ref, w_ref)
    last = reductions[1]
    form_moments(
        dates, lambda b, d, q: r_ref[b, d, :, tile(q)], w_ref, table_ref, s_ref, last.mom,
        lambda b: None, lambda n: last.swap(n).start(),
    )
    spread.drain()
    last.run()
    base = [block_ref[pl.ds(base_row + k, 8, stride=8), :] for k in range(TERMS)]
    answer, variance = solve(last.mine, base)
    own_ref, near_ref, halo_sems = halos[1]
    copies = swap_halo(variance, own_ref, near_ref, halo_sems)
    masks = flip_masks()
    for k in range(TERMS):
        turned = flip(base[k] + answer[k], masks)
        for b in range(BANDS):
            coef_ref[b, k] = (turned if b == 0 else pltpu.roll(turned, 128 - 16 * b, 1))[:, :16]
    last.drain()
    smooth = box_mean(variance, near_ref, copies)
    noise_ref[...] = flip(jnp.sqrt(smooth + EPS), masks)[:, :16]


def reduction_scratch():
    pieces = len(PIECES)
    one, ring = pltpu.SemaphoreType.DMA((pieces,)), pltpu.SemaphoreType.DMA((4, 4, pieces))
    eight = pltpu.SemaphoreType.DMA((8,))
    return [
        *[pltpu.VMEM((SHARDS * count, 128), F32) for _, count in PIECES],
        *[pltpu.VMEM((ZS * count, 128), F32) for _, count in PIECES],
        pltpu.VMEM((4, 4, DEEP, 128), F32),
        pltpu.VMEM((DEEP, 128), F32),
        pltpu.VMEM((8, 128), F32),
        pltpu.VMEM((8, 8, 128), F32),
        one, one, ring, ring, eight, eight,
    ]


def on_device(obs, valid, days):
    dates = obs.shape[1]
    spread = pltpu.SemaphoreType.DMA((4, 4, len(PARTS)))
    own = pltpu.SemaphoreType.DMA((len(PARTS),))
    return pl.pallas_call(
        functools.partial(whole, dates),
        out_shape=(
            jax.ShapeDtypeStruct((BANDS, TERMS, ROWS, 16), F32),
            jax.ShapeDtypeStruct((ROWS, 16), F32),
        ),
        in_specs=[
            pl.BlockSpec(memory_space=pltpu.SMEM),
            pl.BlockSpec(memory_space=pl.ANY),
            pl.BlockSpec(memory_space=pl.ANY),
        ],
        out_specs=(pl.BlockSpec(memory_space=pltpu.VMEM), pl.BlockSpec(memory_space=pltpu.VMEM)),
        scratch_shapes=[
            pltpu.VMEM((BANDS, dates, ROWS, COLS), jnp.bfloat16),
            pltpu.VMEM((dates, ROWS, COLS), jnp.int32),
            pltpu.VMEM((dates * FIELDS, 128), F32),
            pltpu.VMEM((dates, ROWS, COLS), F32),
            pltpu.VMEM((ROWS, COLS), F32),
            pltpu.VMEM((BANDS, dates, ROWS, COLS), F32),
            pltpu.VMEM((SHARDS * BLOCK, 128), F32),
            pltpu.SemaphoreType.DMA((BANDS + 1,)),
            spread, spread, spread, spread, own, own,
            *reduction_scratch(),
            *reduction_scratch(),
        ],
        compiler_params=pltpu.CompilerParams(collective_id=0, has_side_effects=True, vmem_limit_bytes=56 << 20),
    )(days, obs, valid)


def solution(mesh):
    in_specs = (P(None, "date", "space", None), P("date", "space", None), P("date"))
    out_specs = (P(None, None, "space", "date"), P("space", "date"))
    return jax.shard_map(on_device, mesh=mesh, in_specs=in_specs, out_specs=out_specs, check_vma=False)
```

time: 140 us -> 127 us (0.907)
  Pallas kernels: 133 us -> 124 us
  local copies, waits for them, and re-layouts: 5.69 us -> 2.91 us
    pallas_call x4 -> x1, Pallas kernels: 133 us -> 124 us  [on_device(): pl.pallas_call(functools.partial(whole, dates), out_shape=(jax.ShapeDtype...]
    another operation x24 -> x0, local copies, waits for them, and re-layouts: 1.85 us -> none  [the longest x22 1.84 us: design_table(): table = jnp.stack(fields, axis=1)]
    unnamed x8 -> x2, local copies, waits for them, and re-layouts: 3.62 us -> 2.91 us
where the time goes in v2:
time: 127 us
  Pallas kernels  124 us (98%)
  local copies, waits for them, and re-layouts  2.91 us (2%)
    pallas_call x1, Pallas kernels, on_device(): pl.pallas_call(functools.partial(whole, dates), out_shape=(jax.ShapeDtype...  124 us
    unnamed x2, local copies, waits for them, and re-layouts  2.91 us

profile of v2, /device:TPU:1, one launch (start us, length us, event | category | flops | bytes accessed | tf_op | source)
XLA Modules:
  0.0 127.3 jit_solution(10507513540388049438)
XLA Ops:
  0.6 123.7 %shard_map.50 = (f32[7,8,8,16]{3,2,1,0:T(8,128)}, f32[8,16]{1,0:T(8,128)}) custom-call(s32[24]{0:T(128)} %days_ref.1, bf16[7,24,8,512]{3,2,1,0:T(8,128)(2,1)} %obs_hbm.1, s32[24,8,512]{2,1,0:T(8,128)} %valid_hbm.1), custom_call_target="tpu_custom_call" | custom-call | tf_op jit(solution)/shard_map/pallas_call | solution.py:597
  124.4 1.6 %copy.7 = f32[7,8,8,16]{3,2,1,0:T(8,128)} copy(f32[7,8,8,16]{3,2,1,0:T(8,128)} %get-tuple-element.4) | data formatting | bytes 57344
  126.0 1.3 copy.8

commit v3 on v2

v3 whole, which is shorter than its diff:
```python
import functools
import math

import jax
import jax.numpy as jnp
from jax import lax
from jax.experimental import pallas as pl
from jax.experimental.pallas import tpu as pltpu
from jax.sharding import PartitionSpec as P

F32 = jnp.float32
MESH = pl.DeviceIdType.MESH
TUKEY = 4.685
EPS = 1e-06
BANDS = 7
TERMS = 8
ROWS = 8
COLS = 512
WIDE = 256
TILES = 2
SHARDS = 32
DEEP = 80
BLOCK = 64
FIELDS = 24
ZS = 16
UNROLL = 4

C0, S0, TC0, TS0, EXTRA_S = 2, 8, 14, 17, 21
NEIGHBOURS = [(a, b) for a in (-1, 0, 1) for b in (-1, 0, 1) if (a, b) != (0, 0)]
PIECES = ((64, 16), (0, 24), (24, 24), (48, 16))
CHAINS = ((1, 8), (1, 7), (-1, 7), (-1, 6))
SPREADS = ((1, 2, 4), (1, 1, 4), (-1, 1, 4), (-1, 2, 3))
PARTS = ((0, 32), (32, 24), (56, 8))


def extra_row(e):
    return 64 + e if e < 16 else 40 + e


def gram_terms(i, j):
    if i > j:
        i, j = j, i
    if i == 0:
        if j < 2:
            return [(1.0, j)]
        n = j // 2
        return [(1.0, (C0 if j % 2 == 0 else S0) + n)]
    if i == 1:
        if j == 1:
            return [(1.0, 2)]
        n = j // 2
        return [(1.0, (TC0 if j % 2 == 0 else TS0) + n)]
    a, b = i // 2, j // 2

    def cosine(n):
        return 0 if n == 0 else C0 + n

    if i % 2 == 0 and j % 2 == 0:
        return [(0.5, cosine(abs(a - b))), (0.5, cosine(a + b))]
    if i % 2 == 1 and j % 2 == 1:
        return [(0.5, cosine(abs(a - b))), (-0.5, cosine(a + b))]
    s, c = (a, b) if i % 2 == 1 else (b, a)
    terms = [(0.5, S0 + s + c)]
    if s != c:
        terms.append((0.5 if s > c else -0.5, S0 + abs(s - c)))
    return terms


def turn(angle):
    turns = jnp.floor(angle * (0.5 / math.pi) + 0.5)
    half = 0.5 * ((angle - turns * 6.28125) - turns * (2.0 * math.pi - 6.28125))
    square = half * half
    s = jnp.full_like(half, 1.0 / math.factorial(13))
    for n in (11, 9, 7, 5, 3, 1):
        s = s * square + (1.0 if n % 4 == 1 else -1.0) / math.factorial(n)
    s = s * half
    c = jnp.full_like(half, 1.0 / math.factorial(12))
    for n in (10, 8, 6, 4, 2, 0):
        c = c * square + (1.0 if n % 4 == 0 else -1.0) / math.factorial(n)
    return 1.0 - 2.0 * s * s, 2.0 * s * c


def design_table(dates, first_date, day_ref, table_ref):
    day = day_ref[first_date : first_date + dates, :]
    t = (day - 1825.0) / 1825.0
    c1, s1 = turn(day * (2.0 * math.pi / 365.25))
    c, s = [None, c1, 1 - 2 * s1 * s1], [None, s1, 2 * s1 * c1]
    c.append(c1 * c[2] - s1 * s[2])
    s.append(s1 * c[2] + c1 * s[2])
    c += [1 - 2 * s[2] * s[2], c[2] * c[3] - s[2] * s[3], 1 - 2 * s[3] * s[3]]
    s += [2 * s[2] * c[2], s[2] * c[3] + c[2] * s[3], 2 * s[3] * c[3]]
    fields = [jnp.ones_like(t), t, t * t] + c[1:] + s[1:]
    fields += [t * c[h] for h in range(1, 4)] + [t * s[h] for h in range(1, 4)]
    for f, value in enumerate(fields):
        for first in range(0, dates, 8):
            start = (first_date + first) * FIELDS + f
            table_ref[pl.ds(start, 8, stride=FIELDS), :] = value[first : first + 8]


COLUMN = [0, 1, C0 + 1, S0 + 1, C0 + 2, S0 + 2, C0 + 3, S0 + 3]


def flip_masks():
    sub = lax.broadcasted_iota(jnp.int32, (8, 128), 0)
    group = lax.broadcasted_iota(jnp.int32, (8, 128), 1) // 16
    masks = []
    for bit in (4, 2, 1):
        s, g = (sub & bit) != 0, (group & bit) != 0
        masks.append((jnp.logical_and(s, jnp.logical_not(g)), jnp.logical_and(jnp.logical_not(s), g)))
    return masks


def flip(v, masks):
    for bit, (low, high) in zip((4, 2, 1), masks):
        up = pltpu.roll(pltpu.roll(v, bit, 0), 128 - 16 * bit, 1)
        if bit == 4:
            v = jnp.where(jnp.logical_or(low, high), up, v)
        else:
            down = pltpu.roll(pltpu.roll(v, 8 - bit, 0), 16 * bit, 1)
            v = jnp.where(low, up, jnp.where(high, down, v))
    return v


def tile(q):
    return slice(128 * q, 128 * q + 128)


def splat(table_ref, d, field):
    return table_ref[pl.ds(d * FIELDS + field, 8, stride=0), :]


def by_date(dates, one, carry):
    def body(n, carry):
        for u in range(UNROLL):
            carry = one(n * UNROLL + u, carry)
        return carry

    return lax.fori_loop(0, dates // UNROLL, body, carry)


def form_moments(dates, load, w_ref, table_ref, s_ref, out_refs, ready, done):
    masks = flip_masks()
    zero = jnp.zeros((8, 128), F32)

    def put(row, q, v):
        for (first, count), out_ref in zip(PIECES, out_refs):
            if first <= row < first + count:
                out_ref[pl.ds(q * 8 * count + row - first, 8, stride=count), :] = v

    for first in range(0, EXTRA_S, 11):
        fields = list(range(first, min(first + 11, EXTRA_S)))

        def one(d, acc):
            acc = list(acc)
            w = [w_ref[d, :, tile(q)] for q in range(TILES)]
            for n, e in enumerate(fields):
                x = splat(table_ref, d, e) if e else None
                for q in range(TILES):
                    acc[n * TILES + q] = acc[n * TILES + q] + (x * w[q] if e else w[q])
            return tuple(acc)

        acc = by_date(dates, one, (zero,) * (len(fields) * TILES))
        for n, e in enumerate(fields):
            for q in range(TILES):
                put(extra_row(e), q, flip(acc[n * TILES + q], masks))
    done(0)
    for b in range(BANDS):
        ready(b)

        def one(d, carry):
            acc, square = list(carry[0]), list(carry[1])
            wy = []
            for q in range(TILES):
                y = load(b, d, q)
                v = w_ref[d, :, tile(q)] * y
                square[q] = square[q] + v * y
                wy.append(v)
            for k in range(TERMS):
                x = splat(table_ref, d, COLUMN[k]) if k else None
                for q in range(TILES):
                    acc[k * TILES + q] = acc[k * TILES + q] + (x * wy[q] if k else wy[q])
            return tuple(acc), tuple(square)

        acc, square = by_date(dates, one, ((zero,) * (TERMS * TILES), (zero,) * TILES))
        for k in range(TERMS):
            for q in range(TILES):
                put(8 * b + k, q, flip(acc[k * TILES + q], masks))
        for q in range(TILES):
            total = square[q] if b == 0 else s_ref[:, tile(q)] + square[q]
            if b < BANDS - 1:
                s_ref[:, tile(q)] = total
            else:
                put(extra_row(EXTRA_S), q, flip(total, masks))
                for row in range(extra_row(EXTRA_S) + 1, 64):
                    put(row, q, zero)
        for n, (first, count) in enumerate(PIECES):
            if n and 8 * b + 8 == min(first + count, 8 * BANDS):
                done(n)


def form_residuals(dates, obs_ref, mask_ref, table_ref, block_ref, r_ref, w_ref):
    masks = flip_masks()

    def get(row, q):
        return flip(block_ref[pl.ds(q * 8 * BLOCK + row, 8, stride=BLOCK), :], masks)

    for b in range(BANDS):
        beta = [[get(8 * b + k, q) for q in range(TILES)] for k in range(TERMS)]

        def one(d, carry):
            x = [splat(table_ref, d, COLUMN[k]) if k else None for k in range(TERMS)]
            for q in range(TILES):
                fit = beta[0][q]
                for k in range(1, TERMS):
                    fit = fit + x[k] * beta[k][q]
                r = obs_ref[b, d, :, tile(q)].astype(F32) - fit
                r_ref[b, d, :, tile(q)] = r
                if b == 0:
                    w_ref[d, :, tile(q)] = r * r
                else:
                    w_ref[d, :, tile(q)] = w_ref[d, :, tile(q)] + r * r
            return carry

        by_date(dates, one, 0)
    scale = [1.0 / (float(BANDS) * (TUKEY * TUKEY) * (get(8 * BANDS, q) + EPS)) for q in range(TILES)]

    def weigh(d, carry):
        for q in range(TILES):
            left = 1.0 - jnp.minimum(w_ref[d, :, tile(q)] * scale[q], 1.0)
            w_ref[d, :, tile(q)] = mask_ref[d, :, tile(q)] * left * left
        return carry

    by_date(dates, weigh, 0)


def copy_to(src, dst, send, recv, space, date):
    return pltpu.make_async_remote_copy(
        src_ref=src, dst_ref=dst, send_sem=send, recv_sem=recv, device_id=(space, date), device_id_type=MESH
    )


def place():
    s, j = lax.axis_index("space"), lax.axis_index("date")
    return s, j, j // ZS, lax.rem(j, ZS)


def wrap(value, count):
    return lax.rem(value + count, count)


def greet():
    s, j, x, z = place()
    sem = pltpu.get_barrier_semaphore()
    targets = [(s, x * ZS + wrap(z + h, ZS)) for h in (1, -1, 2, -2)] + [(s, (1 - x) * ZS + z)]
    targets += [(wrap(s + a, 16), wrap(j + b, SHARDS)) for a, b in NEIGHBOURS]
    for target in targets:
        pl.semaphore_signal(sem, inc=1, device_id=target, device_id_type=MESH)
    return sem, len(targets)


class Reduction:
    def __init__(self, mom_refs, slot_ref, mine_ref, sems):
        self.mom, self.slot, self.mine = mom_refs, slot_ref, mine_ref
        self.send, self.recv = sems
        self.s, self.j, self.x, self.z = place()

    def length(self, chain):
        return (CHAINS[chain][1] + 1) // 2

    def rows(self, n, chain, step):
        way, first = CHAINS[chain]
        count = PIECES[n][1]
        return pl.ds(pl.multiple_of(wrap(self.z + way * (first - 2 * step), ZS) * count, 8), count)

    def place_of(self, n, chain, step):
        return self.slot.at[chain, step, pl.ds(*PIECES[n])]

    def hop(self, n, chain, step):
        way, first = CHAINS[chain]
        reach = min(2, first - 2 * step)
        source = self.mom[n].at[self.rows(n, chain, 0)] if step == 0 else self.place_of(n, chain, step - 1)
        return copy_to(
            source, self.place_of(n, chain, step), self.send.at[chain, step, n], self.recv.at[chain, step, n],
            self.s, self.x * ZS + wrap(self.z + way * reach, ZS),
        )

    def step(self, n, step):
        for chain in range(4):
            if step >= self.length(chain):
                continue
            if step:
                self.hop(n, chain, step - 1).wait_recv()
                here = self.place_of(n, chain, step - 1)
                here[...] = here[...] + self.mom[n][self.rows(n, chain, step), :]
            self.hop(n, chain, step).start()

    def finish(self, n):
        first, count = PIECES[n]
        total = self.mom[n][pl.ds(pl.multiple_of(self.z * count, 8), count), :]
        for chain in range(4):
            last = self.length(chain) - 1
            self.hop(n, chain, last).wait_recv()
            total = total + self.slot[chain, last, pl.ds(first, count), :]
        self.mine[pl.ds(first, count), :] = total

    def wave(self, wave):
        for n in range(len(PIECES)):
            if 0 <= wave - n < 4:
                self.step(n, wave - n)
            if wave - n == 4:
                self.finish(n)

    def run(self):
        for wave in range(len(PIECES), len(PIECES) + 4):
            self.wave(wave)

    def drain(self):
        for n in range(len(PIECES)):
            for chain in range(4):
                for step in range(self.length(chain)):
                    self.hop(n, chain, step).wait_send()


class Spread:
    def __init__(self, block_ref, sems):
        self.block = block_ref
        self.send, self.recv = sems
        self.s, self.j, self.x, self.z = place()

    def piece(self, owner, n):
        first, count = PARTS[n]
        return self.block.at[pl.ds(pl.multiple_of(wrap(owner + ZS, ZS) * BLOCK + first, 8), count)]

    def offset(self, chain, step):
        way, first, _ = SPREADS[chain]
        return 0 if step == 0 else way * (first + 2 * (step - 1))

    def hop(self, n, chain, step):
        way, first, _ = SPREADS[chain]
        reach = first if step == 0 else 2
        piece = self.piece(self.z - self.offset(chain, step), n)
        return copy_to(
            piece, piece, self.send.at[chain, step, n], self.recv.at[chain, step, n],
            self.s, self.x * ZS + wrap(self.z + way * reach, ZS),
        )

    def arrival(self, n, chain, step):
        piece = self.piece(self.z - self.offset(chain, step + 1), n)
        return copy_to(
            piece, piece, self.send.at[chain, step, n], self.recv.at[chain, step, n], self.s, self.j
        )

    def begin(self, n):
        for chain in range(4):
            self.hop(n, chain, 0).start()

    def relay(self, step):
        for n in range(len(PARTS)):
            for chain in range(4):
                if step <= SPREADS[chain][2]:
                    self.arrival(n, chain, step - 1).wait_recv()
                    if step < SPREADS[chain][2]:
                        self.hop(n, chain, step).start()

    def drain(self):
        for n in range(len(PARTS)):
            for chain in range(4):
                for step in range(SPREADS[chain][2]):
                    self.hop(n, chain, step).wait_send()


def solve(mine_ref, base):
    moment = {}

    def mom(e):
        if e not in moment:
            moment[e] = jnp.broadcast_to(mine_ref[extra_row(e) : extra_row(e) + 1, :], (8, 128))
        return moment[e]

    gram = {}
    for i in range(TERMS):
        for j in range(i, TERMS):
            value = None
            for factor, e in gram_terms(i, j):
                part = mom(e) if factor == 1.0 else factor * mom(e)
                value = part if value is None else value + part
            gram[i, j] = value
    cross = [mine_ref[pl.ds(k, 8, stride=8), :] for k in range(TERMS)]
    work = dict(gram)
    for i in range(TERMS):
        work[i, i] = work[i, i] + 1.0
    right = [cross[k] if base is None else cross[k] - base[k] for k in range(TERMS)]
    inverse, factor = [], {}
    for i in range(TERMS):
        inv = 1.0 / work[i, i]
        inverse.append(inv)
        for r in range(i + 1, TERMS):
            factor[r, i] = work[i, r] * inv
        for r in range(i + 1, TERMS):
            for c in range(r, TERMS):
                work[r, c] = work[r, c] - factor[r, i] * work[i, c]
            right[r] = right[r] - factor[r, i] * right[i]
    answer = [None] * TERMS
    for i in reversed(range(TERMS)):
        value = right[i] * inverse[i]
        for c in range(i + 1, TERMS):
            value = value - factor[c, i] * answer[c]
        answer[i] = value
    lost = None
    for i in range(TERMS):
        image = None
        for c in range(TERMS):
            part = gram[min(i, c), max(i, c)] * answer[c]
            image = part if image is None else image + part
        part = answer[i] * (2.0 * cross[i] - image)
        lost = part if lost is None else lost + part
    sub = lax.broadcasted_iota(jnp.int32, (8, 128), 0)
    lost = jnp.sum(jnp.where(sub < BANDS, lost, 0.0), axis=0, keepdims=True)
    spread = jnp.maximum(mom(EXTRA_S) - jnp.broadcast_to(lost, (8, 128)), 0.0) * (1.0 / BANDS)
    return answer, spread / (1.0 + mom(0))


def swap_halo(variance, own_ref, near_ref, sems):
    send, recv = sems
    s, j, x, z = place()
    own_ref[...] = variance
    copies = []
    for n, (a, b) in enumerate(NEIGHBOURS):
        back = NEIGHBOURS.index((-a, -b))
        copy = copy_to(
            own_ref, near_ref.at[back], send.at[n], recv.at[back], wrap(s + a, 16), wrap(j + b, SHARDS)
        )
        copy.start()
        copies.append(copy)
    return copies


def box_mean(variance, near_ref, copies):
    s, j, x, z = place()
    for copy in copies:
        copy.wait()
    lane = lax.broadcasted_iota(jnp.int32, (8, 128), 1)
    col, row = lane % 16, lane // 16

    def field(a, b):
        if (a, b) == (0, 0):
            return variance
        value = near_ref[NEIGHBOURS.index((a, b))]
        inside = jnp.int32(1)
        if a:
            inside = inside * ((s + a >= 0) & (s + a < 16)).astype(jnp.int32)
        if b:
            inside = inside * ((j + b >= 0) & (j + b < SHARDS)).astype(jnp.int32)
        return jnp.where(jnp.full((8, 128), inside) > 0, value, 0.0)

    across = []
    for a in (-1, 0, 1):
        middle = field(a, 0)
        left = pltpu.roll(field(a, -1), 128 - 16, 1)
        right = pltpu.roll(field(a, 1), 16, 1)
        total = middle
        for step in (1, 2):
            total = total + pltpu.roll(jnp.where(col < step, right, middle), 128 - step, 1)
            total = total + pltpu.roll(jnp.where(col >= 16 - step, left, middle), step, 1)
        across.append(total)
    up, middle, down = across
    total = middle
    for step in (1, 2):
        total = total + pltpu.roll(jnp.where(row < step, down, middle), 128 - 16 * step, 1)
        total = total + pltpu.roll(jnp.where(row >= 8 - step, up, middle), 16 * step, 1)

    def count(index, whole):
        return (jnp.minimum(index + 2, whole - 1) - jnp.maximum(index - 2, 0) + 1).astype(F32)

    return total / (count(s * 8 + row, 128) * count(j * 16 + col, COLS))


def whole(
    dates, days_ref, obs_hbm, valid_hbm, out_ref,
    obs_ref, valid_ref, turned_ref, day_ref, table_ref, mask_ref, w_ref, s_ref, r_ref, block_ref,
    in_sem, trade_send, trade_recv, sp_send, sp_recv, *rest,
):
    s, j, x, z = place()
    own = pl.ds(pl.multiple_of(x * WIDE, 128), WIDE)
    other = pl.ds(pl.multiple_of((1 - x) * WIDE, 128), WIDE)
    early, late = pl.ds(0, dates), pl.ds(dates, dates)
    valid_copies = [
        pltpu.make_async_copy(valid_hbm.at[:, :, cols], valid_ref.at[n], in_sem.at[BANDS + n])
        for n, cols in ((1, other), (0, own))
    ]
    obs_copies = [
        pltpu.make_async_copy(obs_hbm.at[b, :, :, own], obs_ref.at[b, early], in_sem.at[b]) for b in range(BANDS)
    ]
    for copy in valid_copies + obs_copies:
        copy.start()
    barrier, guests = greet()
    partner = (s, (1 - x) * ZS + z)

    def trade(n, src, dst):
        return copy_to(src, dst, trade_send.at[n], trade_recv.at[n], *partner)

    trades = [
        trade(b, obs_hbm.at[b, :, :, other], obs_ref.at[b, late]) for b in range(BANDS)
    ]
    day_trade = trade(BANDS, day_ref.at[early], day_ref.at[late])
    mask_trade = trade(BANDS + 1, turned_ref.at[0], turned_ref.at[1])
    rows = lax.broadcasted_iota(jnp.int32, (dates, 128), 0)
    day = jnp.zeros((dates, 128), F32)
    for d in range(dates):
        day = jnp.where(rows == d, days_ref[d].astype(F32), day)
    day_ref[0:dates, :] = day
    valid_copies[0].wait()

    @pl.loop(0, dates)
    def _(d):
        turned_ref[0, d] = valid_ref[1, d].astype(F32).astype(jnp.bfloat16)

    design_table(dates, 0, day_ref, table_ref)
    pl.semaphore_wait(barrier, guests)
    day_trade.start()
    mask_trade.start()
    for copy in trades:
        copy.start()
    valid_copies[1].wait()

    @pl.loop(0, dates)
    def _(d):
        mask_ref[d] = valid_ref[0, d].astype(F32)

    day_trade.wait_recv()
    design_table(dates, dates, day_ref, table_ref)
    mask_trade.wait_recv()

    @pl.loop(0, dates)
    def _(d):
        mask_ref[dates + d] = turned_ref[1, d].astype(F32)

    reductions, halos = [], []
    for n in range(2):
        part = rest[12 * n : 12 * n + 12]
        reductions.append(Reduction(part[:4], part[4], part[5], part[8:10]))
        halos.append((part[6], part[7], part[10:12]))

    def ready(b):
        obs_copies[b].wait()
        trades[b].wait_recv()

    both = 2 * dates
    first, last = reductions
    form_moments(
        both, lambda b, d, q: obs_ref[b, d, :, tile(q)].astype(F32), mask_ref, table_ref, s_ref, first.mom,
        ready, first.wave,
    )
    first.run()
    answer, variance = solve(first.mine, None)
    own_ref, near_ref, halo_sems = halos[0]
    copies = swap_halo(variance, own_ref, near_ref, halo_sems)
    base_row = pl.multiple_of(z * BLOCK, 8)
    for k in range(TERMS):
        block_ref[pl.ds(base_row + k, 8, stride=8), :] = answer[k]
    spread = Spread(block_ref, (sp_send, sp_recv))
    spread.begin(0)
    spread.begin(1)
    smooth = box_mean(variance, near_ref, copies)
    block_ref[pl.ds(pl.multiple_of(base_row + 8 * BANDS, 8), 8), :] = smooth
    spread.begin(2)
    for step in range(1, 5):
        spread.relay(step)
    form_residuals(both, obs_ref, mask_ref, table_ref, block_ref, r_ref, w_ref)
    form_moments(
        both, lambda b, d, q: r_ref[b, d, :, tile(q)], w_ref, table_ref, s_ref, last.mom,
        lambda b: None, last.wave,
    )
    spread.drain()
    first.drain()
    for copy in trades + [day_trade, mask_trade]:
        copy.wait_send()
    last.run()
    base = [block_ref[pl.ds(base_row + k, 8, stride=8), :] for k in range(TERMS)]
    answer, variance = solve(last.mine, base)
    own_ref, near_ref, halo_sems = halos[1]
    copies = swap_halo(variance, own_ref, near_ref, halo_sems)
    masks = flip_masks()
    for k in range(TERMS):
        turned = flip(base[k] + answer[k], masks)
        for b in range(BANDS):
            out_ref[b * TERMS + k] = (turned if b == 0 else pltpu.roll(turned, 128 - 16 * b, 1))[:, :16]
    last.drain()
    smooth = box_mean(variance, near_ref, copies)
    out_ref[BANDS * TERMS] = flip(jnp.sqrt(smooth + EPS), masks)[:, :16]


def reduction_scratch():
    ring, eight = pltpu.SemaphoreType.DMA((4, 4, len(PIECES))), pltpu.SemaphoreType.DMA((8,))
    return [
        *[pltpu.VMEM((ZS * count, 128), F32) for _, count in PIECES],
        pltpu.VMEM((4, 4, DEEP, 128), F32),
        pltpu.VMEM((DEEP, 128), F32),
        pltpu.VMEM((8, 128), F32),
        pltpu.VMEM((8, 8, 128), F32),
        ring, ring, eight, eight,
    ]


def on_device(obs, valid, days):
    dates = obs.shape[1]
    spread = pltpu.SemaphoreType.DMA((4, 4, len(PARTS)))
    trade = pltpu.SemaphoreType.DMA((BANDS + 2,))
    out = pl.pallas_call(
        functools.partial(whole, dates),
        out_shape=jax.ShapeDtypeStruct((BANDS * TERMS + 1, ROWS, 16), F32),
        in_specs=[
            pl.BlockSpec(memory_space=pltpu.SMEM),
            pl.BlockSpec(memory_space=pl.ANY),
            pl.BlockSpec(memory_space=pl.ANY),
        ],
        out_specs=pl.BlockSpec(memory_space=pltpu.VMEM),
        scratch_shapes=[
            pltpu.VMEM((BANDS, 2 * dates, ROWS, WIDE), jnp.bfloat16),
            pltpu.VMEM((2, dates, ROWS, WIDE), jnp.int32),
            pltpu.VMEM((2, dates, ROWS, WIDE), jnp.bfloat16),
            pltpu.VMEM((2 * dates, 128), F32),
            pltpu.VMEM((2 * dates * FIELDS, 128), F32),
            pltpu.VMEM((2 * dates, ROWS, WIDE), F32),
            pltpu.VMEM((2 * dates, ROWS, WIDE), F32),
            pltpu.VMEM((ROWS, WIDE), F32),
            pltpu.VMEM((BANDS, 2 * dates, ROWS, WIDE), F32),
            pltpu.VMEM((ZS * BLOCK, 128), F32),
            pltpu.SemaphoreType.DMA((BANDS + 2,)),
            trade, trade, spread, spread,
            *reduction_scratch(),
            *reduction_scratch(),
        ],
        compiler_params=pltpu.CompilerParams(collective_id=0, has_side_effects=True, vmem_limit_bytes=56 << 20),
    )(days, obs, valid)
    return out[: BANDS * TERMS].reshape(BANDS, TERMS, ROWS, 16), out[BANDS * TERMS]


def solution(mesh):
    in_specs = (P(None, "date", "space", None), P("date", "space", None), P("date"))
    out_specs = (P(None, None, "space", "date"), P("space", "date"))
    return jax.shard_map(on_device, mesh=mesh, in_specs=in_specs, out_specs=out_specs, check_vma=False)
```

time: 127 us -> 119 us (0.937)
  Pallas kernels: 124 us -> 115 us
    pallas_call x1, Pallas kernels: 124 us -> 115 us  [on_device(): pl.pallas_call(functools.partial(whole, dates), out_shape=jax.ShapeDtypeS...]
    unnamed x2 -> x0, local copies, waits for them, and re-layouts: 2.91 us -> none
    slice x0 -> x1, local copies, waits for them, and re-layouts: none -> 1.64 us  [on_device(): out[:BANDS * TERMS].reshape(BANDS, TERMS, ROWS, 16)]
where the time goes in v3:
time: 119 us
  Pallas kernels  115 us (97%)
  local copies, waits for them, and re-layouts  2.91 us (2%)
    pallas_call x1, Pallas kernels, on_device(): pl.pallas_call(functools.partial(whole, dates), out_shape=jax.ShapeDtypeS...  115 us

profile of v3, /device:TPU:1, one launch (start us, length us, event | category | flops | bytes accessed | tf_op | source)
XLA Modules:
  0.0 119.0 jit_solution(6238261942329249610)
XLA Ops:
  0.6 115.5 %shard_map.50 = f32[57,8,16]{2,1,0:T(8,128)} custom-call(s32[24]{0:T(128)} %days_ref.1, bf16[7,24,8,512]{3,2,1,0:T(8,128)(2,1)} %obs_hbm.1, s32[24,8,512]{2,1,0:T(8,128)} %valid_hbm.1), custom_call_target="tpu_custom_call" | custom-call | tf_op jit(solution)/shard_map/pallas_call | solution.py:609
  116.1 1.3 %slice_bitcast_fusion = f32[8,16]{1,0:T(8,128)} fusion(f32[57,8,16]{2,1,0:T(8,128)} %shard_map.50), kind=kLoop, calls=%fused_computation | loop fusion | bytes 1024 | tf_op jit(solution)/shard_map/squeeze | solution.py:636
  117.4 1.6 %slice.6 = f32[56,8,16]{2,1,0:T(8,128)} slice(f32[57,8,16]{2,1,0:T(8,128)} %shard_map.50), slice={[0:56], [0:8], [0:16]} | slice | bytes 57344 | tf_op jit(solution)/shard_map/slice | solution.py:636

commit v4 on v3

--- a/solution.py
+++ b/solution.py
@@ -27,9 +27,27 @@
 
 C0, S0, TC0, TS0, EXTRA_S = 2, 8, 14, 17, 21
 NEIGHBOURS = [(a, b) for a in (-1, 0, 1) for b in (-1, 0, 1) if (a, b) != (0, 0)]
-PIECES = ((64, 16), (0, 24), (24, 24), (48, 16))
-CHAINS = ((1, 8), (1, 7), (-1, 7), (-1, 6))
-SPREADS = ((1, 2, 4), (1, 1, 4), (-1, 1, 4), (-1, 2, 3))
+PIECES = ((64, 16), (0, 16), (16, 24), (40, 24))
+BY_TWO = ((1, 8, 2), (1, 7, 2), (-1, 7, 2), (-1, 6, 2))
+BY_FOUR = tuple((1, n, 4) for n in (8, 7, 6, 5)) + tuple((-1, n, 4) for n in (7, 6, 5, 4))
+CHAINS = (BY_TWO, BY_TWO, BY_TWO, BY_FOUR)
+SLOW_PLAN = (
+    ((0, 0),),
+    ((1, 0), (0, 1)),
+    ((2, 0), (1, 1), (0, 2)),
+    ((3, 0),),
+    ((0, 3), (1, 2), (2, 1), (0, 4), (1, 3), (2, 2), (3, 1), (1, 4), (2, 3), (3, 2), (2, 4)),
+)
+FAST_PLAN = (
+    ((0, 0),),
+    ((1, 0),),
+    ((2, 0),),
+    ((3, 0),),
+    ((0, 1), (1, 1), (2, 1), (0, 2), (1, 2), (3, 1), (2, 2), (0, 3), (1, 3), (2, 3), (0, 4), (1, 4), (3, 2), (2, 4)),
+)
+OUT_BY_TWO = ((1, 2, 4, 2), (1, 1, 4, 2), (-1, 1, 4, 2), (-1, 2, 3, 2))
+OUT_BY_FOUR = tuple((1, n, 2, 4) for n in (4, 3, 2, 1)) + tuple((-1, n, 2 if n < 4 else 1, 4) for n in (4, 3, 2, 1))
+SPREADS = (OUT_BY_TWO, OUT_BY_TWO, OUT_BY_FOUR)
 PARTS = ((0, 32), (32, 24), (56, 8))
 
 
@@ -198,7 +216,7 @@
                 done(n)
 
 
-def form_residuals(dates, obs_ref, mask_ref, table_ref, block_ref, r_ref, w_ref):
+def form_residuals(dates, obs_ref, mask_ref, table_ref, block_ref, r_ref, w_ref, smooth_ready):
     masks = flip_masks()
 
     def get(row, q):
@@ -222,6 +240,7 @@
             return carry
 
         by_date(dates, one, 0)
+    smooth_ready()
     scale = [1.0 / (float(BANDS) * (TUKEY * TUKEY) * (get(8 * BANDS, q) + EPS)) for q in range(TILES)]
 
     def weigh(d, carry):
@@ -251,7 +270,7 @@
 def greet():
     s, j, x, z = place()
     sem = pltpu.get_barrier_semaphore()
-    targets = [(s, x * ZS + wrap(z + h, ZS)) for h in (1, -1, 2, -2)] + [(s, (1 - x) * ZS + z)]
+    targets = [(s, x * ZS + wrap(z + h, ZS)) for h in (1, -1, 2, -2, 3, -3, 4, -4)] + [(s, (1 - x) * ZS + z)]
     targets += [(wrap(s + a, 16), wrap(j + b, SHARDS)) for a, b in NEIGHBOURS]
     for target in targets:
         pl.semaphore_signal(sem, inc=1, device_id=target, device_id_type=MESH)
@@ -259,25 +278,26 @@
 
 
 class Reduction:
-    def __init__(self, mom_refs, slot_ref, mine_ref, sems):
-        self.mom, self.slot, self.mine = mom_refs, slot_ref, mine_ref
+    def __init__(self, mom_refs, slot_ref, mine_ref, sems, plan):
+        self.mom, self.slot, self.mine, self.plan = mom_refs, slot_ref, mine_ref, plan
         self.send, self.recv = sems
         self.s, self.j, self.x, self.z = place()
 
-    def length(self, chain):
-        return (CHAINS[chain][1] + 1) // 2
+    def length(self, n, chain):
+        _, first, stride = CHAINS[n][chain]
+        return (first + stride - 1) // stride
 
     def rows(self, n, chain, step):
-        way, first = CHAINS[chain]
+        way, first, stride = CHAINS[n][chain]
         count = PIECES[n][1]
-        return pl.ds(pl.multiple_of(wrap(self.z + way * (first - 2 * step), ZS) * count, 8), count)
+        return pl.ds(pl.multiple_of(wrap(self.z + way * (first - stride * step), ZS) * count, 8), count)
 
     def place_of(self, n, chain, step):
         return self.slot.at[chain, step, pl.ds(*PIECES[n])]
 
     def hop(self, n, chain, step):
-        way, first = CHAINS[chain]
-        reach = min(2, first - 2 * step)
+        way, first, stride = CHAINS[n][chain]
+        reach = min(stride, first - stride * step)
         source = self.mom[n].at[self.rows(n, chain, 0)] if step == 0 else self.place_of(n, chain, step - 1)
         return copy_to(
             source, self.place_of(n, chain, step), self.send.at[chain, step, n], self.recv.at[chain, step, n],
@@ -285,8 +305,8 @@
         )
 
     def step(self, n, step):
-        for chain in range(4):
-            if step >= self.length(chain):
+        for chain in range(len(CHAINS[n])):
+            if step >= self.length(n, chain):
                 continue
             if step:
                 self.hop(n, chain, step - 1).wait_recv()
@@ -297,27 +317,26 @@
     def finish(self, n):
         first, count = PIECES[n]
         total = self.mom[n][pl.ds(pl.multiple_of(self.z * count, 8), count), :]
-        for chain in range(4):
-            last = self.length(chain) - 1
+        for chain in range(len(CHAINS[n])):
+            last = self.length(n, chain) - 1
             self.hop(n, chain, last).wait_recv()
             total = total + self.slot[chain, last, pl.ds(first, count), :]
         self.mine[pl.ds(first, count), :] = total
 
-    def wave(self, wave):
-        for n in range(len(PIECES)):
-            if 0 <= wave - n < 4:
-                self.step(n, wave - n)
-            if wave - n == 4:
+    def advance(self, stage):
+        for n, step in self.plan[stage]:
+            if step == max(self.length(n, chain) for chain in range(len(CHAINS[n]))):
                 self.finish(n)
+            else:
+                self.step(n, step)
 
     def run(self):
-        for wave in range(len(PIECES), len(PIECES) + 4):
-            self.wave(wave)
+        self.advance(len(PIECES))
 
     def drain(self):
         for n in range(len(PIECES)):
-            for chain in range(4):
-                for step in range(self.length(chain)):
+            for chain in range(len(CHAINS[n])):
+                for step in range(self.length(n, chain)):
                     self.hop(n, chain, step).wait_send()
 
 
@@ -331,41 +350,40 @@
         first, count = PARTS[n]
         return self.block.at[pl.ds(pl.multiple_of(wrap(owner + ZS, ZS) * BLOCK + first, 8), count)]
 
-    def offset(self, chain, step):
-        way, first, _ = SPREADS[chain]
-        return 0 if step == 0 else way * (first + 2 * (step - 1))
+    def offset(self, n, chain, step):
+        way, first, _, stride = SPREADS[n][chain]
+        return 0 if step == 0 else way * (first + stride * (step - 1))
 
     def hop(self, n, chain, step):
-        way, first, _ = SPREADS[chain]
-        reach = first if step == 0 else 2
-        piece = self.piece(self.z - self.offset(chain, step), n)
+        way, first, _, stride = SPREADS[n][chain]
+        reach = first if step == 0 else stride
+        piece = self.piece(self.z - self.offset(n, chain, step), n)
         return copy_to(
             piece, piece, self.send.at[chain, step, n], self.recv.at[chain, step, n],
             self.s, self.x * ZS + wrap(self.z + way * reach, ZS),
         )
 
     def arrival(self, n, chain, step):
-        piece = self.piece(self.z - self.offset(chain, step + 1), n)
+        piece = self.piece(self.z - self.offset(n, chain, step + 1), n)
         return copy_to(
             piece, piece, self.send.at[chain, step, n], self.recv.at[chain, step, n], self.s, self.j
         )
 
     def begin(self, n):
-        for chain in range(4):
+        for chain in range(len(SPREADS[n])):
             self.hop(n, chain, 0).start()
 
-    def relay(self, step):
-        for n in range(len(PARTS)):
-            for chain in range(4):
-                if step <= SPREADS[chain][2]:
-                    self.arrival(n, chain, step - 1).wait_recv()
-                    if step < SPREADS[chain][2]:
-                        self.hop(n, chain, step).start()
+    def relay(self, n, step):
+        for chain in range(len(SPREADS[n])):
+            if step <= SPREADS[n][chain][2]:
+                self.arrival(n, chain, step - 1).wait_recv()
+                if step < SPREADS[n][chain][2]:
+                    self.hop(n, chain, step).start()
 
     def drain(self):
         for n in range(len(PARTS)):
-            for chain in range(4):
-                for step in range(SPREADS[chain][2]):
+            for chain in range(len(SPREADS[n])):
+                for step in range(SPREADS[n][chain][2]):
                     self.hop(n, chain, step).wait_send()
 
 
@@ -538,7 +556,7 @@
     reductions, halos = [], []
     for n in range(2):
         part = rest[12 * n : 12 * n + 12]
-        reductions.append(Reduction(part[:4], part[4], part[5], part[8:10]))
+        reductions.append(Reduction(part[:4], part[4], part[5], part[8:10], (SLOW_PLAN, FAST_PLAN)[n]))
         halos.append((part[6], part[7], part[10:12]))
 
     def ready(b):
@@ -549,7 +567,7 @@
     first, last = reductions
     form_moments(
         both, lambda b, d, q: obs_ref[b, d, :, tile(q)].astype(F32), mask_ref, table_ref, s_ref, first.mom,
-        ready, first.wave,
+        ready, first.advance,
     )
     first.run()
     answer, variance = solve(first.mine, None)
@@ -561,20 +579,20 @@
     spread = Spread(block_ref, (sp_send, sp_recv))
     spread.begin(0)
     spread.begin(1)
+    spread.relay(0, 1)
+    spread.relay(1, 1)
     smooth = box_mean(variance, near_ref, copies)
     block_ref[pl.ds(pl.multiple_of(base_row + 8 * BANDS, 8), 8), :] = smooth
     spread.begin(2)
-    for step in range(1, 5):
-        spread.relay(step)
-    form_residuals(both, obs_ref, mask_ref, table_ref, block_ref, r_ref, w_ref)
+    for n, step in ((0, 2), (1, 2), (0, 3), (1, 3), (2, 1), (0, 4), (1, 4)):
+        spread.relay(n, step)
+    form_residuals(
+        both, obs_ref, mask_ref, table_ref, block_ref, r_ref, w_ref, lambda: spread.relay(2, 2)
+    )
     form_moments(
         both, lambda b, d, q: r_ref[b, d, :, tile(q)], w_ref, table_ref, s_ref, last.mom,
-        lambda b: None, last.wave,
+        lambda b: None, last.advance,
     )
-    spread.drain()
-    first.drain()
-    for copy in trades + [day_trade, mask_trade]:
-        copy.wait_send()
     last.run()
     base = [block_ref[pl.ds(base_row + k, 8, stride=8), :] for k in range(TERMS)]
     answer, variance = solve(last.mine, base)
@@ -585,16 +603,20 @@
         turned = flip(base[k] + answer[k], masks)
         for b in range(BANDS):
             out_ref[b * TERMS + k] = (turned if b == 0 else pltpu.roll(turned, 128 - 16 * b, 1))[:, :16]
+    spread.drain()
+    first.drain()
     last.drain()
+    for copy in trades + [day_trade, mask_trade]:
+        copy.wait_send()
     smooth = box_mean(variance, near_ref, copies)
     out_ref[BANDS * TERMS] = flip(jnp.sqrt(smooth + EPS), masks)[:, :16]
 
 
 def reduction_scratch():
-    ring, eight = pltpu.SemaphoreType.DMA((4, 4, len(PIECES))), pltpu.SemaphoreType.DMA((8,))
+    ring, eight = pltpu.SemaphoreType.DMA((8, 4, len(PIECES))), pltpu.SemaphoreType.DMA((8,))
     return [
         *[pltpu.VMEM((ZS * count, 128), F32) for _, count in PIECES],
-        pltpu.VMEM((4, 4, DEEP, 128), F32),
+        pltpu.VMEM((8, 4, DEEP, 128), F32),
         pltpu.VMEM((DEEP, 128), F32),
         pltpu.VMEM((8, 128), F32),
         pltpu.VMEM((8, 8, 128), F32),
@@ -604,7 +626,7 @@
 
 def on_device(obs, valid, days):
     dates = obs.shape[1]
-    spread = pltpu.SemaphoreType.DMA((4, 4, len(PARTS)))
+    spread = pltpu.SemaphoreType.DMA((8, 4, len(PARTS)))
     trade = pltpu.SemaphoreType.DMA((BANDS + 2,))
     out = pl.pallas_call(
         functools.partial(whole, dates),

time: 119 us -> 111 us (0.933)
  Pallas kernels: 115 us -> 107 us
    pallas_call x1, Pallas kernels: 115 us -> 107 us  [on_device(): pl.pallas_call(functools.partial(whole, dates), out_shape=jax.ShapeDtypeS...]
where the time goes in v4:
time: 111 us
  Pallas kernels  107 us (96%)
  local copies, waits for them, and re-layouts  2.91 us (3%)
    pallas_call x1, Pallas kernels, on_device(): pl.pallas_call(functools.partial(whole, dates), out_shape=jax.ShapeDtypeS...  107 us

profile of v4, /device:TPU:1, one launch (start us, length us, event | category | flops | bytes accessed | tf_op | source)
XLA Modules:
  0.0 111.0 jit_solution(1915310432570610616)
XLA Ops:
  0.6 107.5 %shard_map.50 = f32[57,8,16]{2,1,0:T(8,128)} custom-call(s32[24]{0:T(128)} %days_ref.1, bf16[7,24,8,512]{3,2,1,0:T(8,128)(2,1)} %obs_hbm.1, s32[24,8,512]{2,1,0:T(8,128)} %valid_hbm.1), custom_call_target="tpu_custom_call" | custom-call | tf_op jit(solution)/shard_map/pallas_call | solution.py:631
  108.1 1.3 %slice_bitcast_fusion = f32[8,16]{1,0:T(8,128)} fusion(f32[57,8,16]{2,1,0:T(8,128)} %shard_map.50), kind=kLoop, calls=%fused_computation | loop fusion | bytes 1024 | tf_op jit(solution)/shard_map/squeeze | solution.py:658
  109.4 1.6 %slice.6 = f32[56,8,16]{2,1,0:T(8,128)} slice(f32[57,8,16]{2,1,0:T(8,128)} %shard_map.50), slice={[0:56], [0:8], [0:16]} | slice | bytes 57344 | tf_op jit(solution)/shard_map/slice | solution.py:658

commit v5 on v4

--- a/solution.py
+++ b/solution.py
@@ -23,7 +23,7 @@
 BLOCK = 64
 FIELDS = 24
 ZS = 16
-UNROLL = 4
+UNROLL = 8
 
 C0, S0, TC0, TS0, EXTRA_S = 2, 8, 14, 17, 21
 NEIGHBOURS = [(a, b) for a in (-1, 0, 1) for b in (-1, 0, 1) if (a, b) != (0, 0)]
@@ -612,6 +612,12 @@
     out_ref[BANDS * TERMS] = flip(jnp.sqrt(smooth + EPS), masks)[:, :16]
 
 
+def part_outputs(out_ref, coef_ref, noise_ref):
+    for b in range(BANDS):
+        coef_ref[b] = out_ref[b * TERMS : (b + 1) * TERMS]
+    noise_ref[...] = out_ref[BANDS * TERMS]
+
+
 def reduction_scratch():
     ring, eight = pltpu.SemaphoreType.DMA((8, 4, len(PIECES))), pltpu.SemaphoreType.DMA((8,))
     return [
@@ -655,7 +661,15 @@
         ],
         compiler_params=pltpu.CompilerParams(collective_id=0, has_side_effects=True, vmem_limit_bytes=56 << 20),
     )(days, obs, valid)
-    return out[: BANDS * TERMS].reshape(BANDS, TERMS, ROWS, 16), out[BANDS * TERMS]
+    return pl.pallas_call(
+        part_outputs,
+        out_shape=(
+            jax.ShapeDtypeStruct((BANDS, TERMS, ROWS, 16), F32),
+            jax.ShapeDtypeStruct((ROWS, 16), F32),
+        ),
+        in_specs=[pl.BlockSpec(memory_space=pltpu.VMEM)],
+        out_specs=(pl.BlockSpec(memory_space=pltpu.VMEM), pl.BlockSpec(memory_space=pltpu.VMEM)),
+    )(out)
 
 
 def solution(mesh):

time: 111 us -> 109 us (0.982)
  local copies, waits for them, and re-layouts: 2.91 us -> 0 us
    pallas_call x0 -> x1, Pallas kernels: none -> 1.65 us  [on_device(): pl.pallas_call(part_outputs, out_shape=(jax.ShapeDtypeStruct((BANDS, TERM...]
    slice x1 -> x0, local copies, waits for them, and re-layouts: 1.64 us -> none  [on_device(): out[:BANDS * TERMS].reshape(BANDS, TERMS, ROWS, 16)]
    squeeze x1 -> x0, local copies, waits for them, and re-layouts: 1.27 us -> none  [on_device(): out[BANDS * TERMS]]
where the time goes in v5:
time: 109 us
  Pallas kernels  108 us (99%)
    pallas_call x1, Pallas kernels, on_device(): pl.pallas_call(functools.partial(whole, dates), out_shape=jax.ShapeDtypeS...  107 us

profile of v5, /device:TPU:1, one launch (start us, length us, event | category | flops | bytes accessed | tf_op | source)
XLA Modules:
  0.0 108.9 jit_solution(14612095139290011483)
XLA Ops:
  0.6 106.6 %shard_map.50.out_ref = f32[57,8,16]{2,1,0:T(8,128)} custom-call(s32[24]{0:T(128)} %days_ref.1, bf16[7,24,8,512]{3,2,1,0:T(8,128)(2,1)} %obs_hbm.1, s32[24,8,512]{2,1,0:T(8,128)} %valid_hbm.1), custom_call_target="tpu_custom_call" | custom-call | tf_op jit(solution)/shard_map/pallas_call | solution.py:637
  107.3 1.6 %shard_map.51 = (f32[7,8,8,16]{3,2,1,0:T(8,128)}, f32[8,16]{1,0:T(8,128)}) custom-call(f32[57,8,16]{2,1,0:T(8,128)} %shard_map.50.out_ref), custom_call_target="tpu_custom_call" | custom-call | tf_op jit(solution)/shard_map/pallas_call | solution.py:664

commit v6 on v5

--- a/solution.py
+++ b/solution.py
@@ -23,7 +23,7 @@
 BLOCK = 64
 FIELDS = 24
 ZS = 16
-UNROLL = 8
+UNROLL = 16
 
 C0, S0, TC0, TS0, EXTRA_S = 2, 8, 14, 17, 21
 NEIGHBOURS = [(a, b) for a in (-1, 0, 1) for b in (-1, 0, 1) if (a, b) != (0, 0)]

time: 109 us -> 109 us (level)
  no operation moved by 1% of the time
where the time goes in v6:
time: 109 us
  Pallas kernels  108 us (99%)
    pallas_call x1, Pallas kernels, on_device(): pl.pallas_call(functools.partial(whole, dates), out_shape=jax.ShapeDtypeS...  106 us

profile of v6, /device:TPU:1, one launch (start us, length us, event | category | flops | bytes accessed | tf_op | source)
XLA Modules:
  0.0 108.7 jit_solution(6614715274758234100)
XLA Ops:
  0.6 106.4 %shard_map.50.out_ref = f32[57,8,16]{2,1,0:T(8,128)} custom-call(s32[24]{0:T(128)} %days_ref.1, bf16[7,24,8,512]{3,2,1,0:T(8,128)(2,1)} %obs_hbm.1, s32[24,8,512]{2,1,0:T(8,128)} %valid_hbm.1), custom_call_target="tpu_custom_call" | custom-call | tf_op jit(solution)/shard_map/pallas_call | solution.py:637
  107.0 1.6 %shard_map.51 = (f32[7,8,8,16]{3,2,1,0:T(8,128)}, f32[8,16]{1,0:T(8,128)}) custom-call(f32[57,8,16]{2,1,0:T(8,128)} %shard_map.50.out_ref), custom_call_target="tpu_custom_call" | custom-call | tf_op jit(solution)/shard_map/pallas_call | solution.py:664
